TPU v7x, 128 devices: a whole 4x4x4 slice. The times are simulated.
128 devices in a mesh: owner: 16 (over y, z), kvh: 8 (over x, core).
Axes of the slice: x: 4, y: 4, z: 4, core: 2. Of those that a mesh axis runs over, the one named last changes fastest.
Arguments:
- queries: bfloat16 [32, 32, 64, 128], P('owner', None, 'kvh'), may hold values from -6 to 6
- new_keys: bfloat16 [32, 32, 8, 128], P('owner', None, 'kvh'), may hold values from -6 to 6
- new_values: bfloat16 [32, 32, 8, 128], P('owner', None, 'kvh'), may hold values from -6 to 6
- ancestors: int32 [32, 32], P('owner'), may hold values from 0 to 95, as said below
- tile_keys: bfloat16 [96, 8, 512, 128], P('owner', 'kvh'), may hold values from -6 to 6
- tile_values: bfloat16 [96, 8, 512, 128], P('owner', 'kvh'), may hold values from -6 to 6
- tile_lengths: int32 [96], P('owner'), may hold values from 2 to 512
- out_weight: bfloat16 [8192, 8192], P('kvh'), may hold values from -0.0625 to 0.0625
Outputs:
- mixed: bfloat16 [1024, 8192], P(('owner', 'kvh'))
Inputs may be any that keep to these rules, and one draw needn't show every extreme that they name: `ancestors`: each row names 32 different tiles.
All inputs are finite; a program needn't handle non-finite values.
Results may differ from a plain program's by a relative error of at most 0.017.
Values may be sent and summed in bfloat16 or wider, within the bound.
No kernel may reach another device: no remote copies, remote signals or barrier semaphores. Data moves between devices by JAX's collectives and lax.ppermute only.
A program may use at most 320 MiB of HBM per device.

v0:
```python
import functools
import math

import jax
import jax.numpy as jnp
from jax import lax
from jax.experimental import pallas as pl
from jax.experimental.pallas import tpu as pltpu
from jax.sharding import PartitionSpec as P

NEG = -1e30
META = 16
STEP = 256
F32 = jnp.float32
BF16 = jnp.bfloat16
VMEM = pl.BlockSpec(memory_space=pltpu.VMEM)
SMEM = pl.BlockSpec(memory_space=pltpu.SMEM)
ANY = pl.BlockSpec(memory_space=pl.ANY)
LOG2 = 1.0 / math.log(2.0)


def to_lanes(column, count):
    r = lax.broadcasted_iota(jnp.int32, (128, 128), 0)
    c = lax.broadcasted_iota(jnp.int32, (128, 128), 1)
    eye = r == c
    rows = []
    for b in range(count // 128):
        rows.append(jnp.sum(jnp.where(eye, column[b * 128 : (b + 1) * 128], 0.0), axis=0, keepdims=True))
    return rows


def in_parts(lines):
    pieces = []
    for line in lines:
        high = line.astype(BF16).astype(F32)
        mid = (line - high).astype(BF16).astype(F32)
        pieces += [high, mid, line - high - mid]
    pad = jnp.zeros((META - len(pieces), 128), F32)
    return jnp.concatenate(pieces + [pad], axis=0).astype(BF16)


def levels(meta, b):
    return meta[3 * b : 3 * b + 1] + meta[3 * b + 1 : 3 * b + 2] + meta[3 * b + 2 : 3 * b + 3]


def prepare_kernel(scale, group, lengths, *refs):
    given, (kt_ref, va_ref, o_ref), held, sems = refs[:5], refs[5:8], refs[8:13], refs[13:]
    copies = [pltpu.make_async_copy(a, b, sem) for a, b, sem in zip(given, held, sems)]
    for copy in copies:
        copy.start()
    q_ref, nk_ref, nv_ref, k_ref, v_ref = held
    tiles, size, width = k_ref.shape
    for copy in copies:
        copy.wait()

    @pl.loop(0, tiles)
    def _(t):
        live = lax.broadcasted_iota(jnp.int32, (size, width), 0) < lengths[t]
        k = k_ref[t].astype(F32)
        kt_ref[t] = jnp.where(live, k, k[:1]).T.astype(BF16)
        va_ref[t, :, :width] = jnp.where(live, v_ref[t].astype(F32), 0.0).astype(BF16)
        va_ref[t, :, width:] = live.astype(F32).astype(BF16)

    halves, part, _ = q_ref.shape
    new = nk_ref.shape[1]
    rows = halves * part
    for i in range(halves):
        s = lax.dot_general(q_ref[i], nk_ref[i], (((1,), (1,)), ((), ())), preferred_element_type=F32)
        token = lax.broadcasted_iota(jnp.int32, (part, new), 0) // group
        seen = token >= lax.broadcasted_iota(jnp.int32, (part, new), 1)
        s = jnp.where(seen, s, NEG)
        peak = jnp.max(s, axis=1, keepdims=True)
        weights = jnp.where(seen, jnp.exp2((s - peak) * scale), 0.0)
        total = jnp.sum(weights, axis=1, keepdims=True)
        summed = jnp.dot(weights.astype(BF16), nv_ref[i], preferred_element_type=F32)
        o_ref[i * part : (i + 1) * part, :] = summed / total
        level = peak * scale + jnp.log(total) * LOG2
        rowed = to_lanes(jnp.broadcast_to(level, (part, width)), part)
        for b, line in enumerate(rowed):
            at = rows + i * len(rowed) + b
            o_ref[at : at + 1, :] = line


def prepare(lengths, q, new_keys, new_values, keys, values, scale, group):
    halves, part, width = q.shape
    tiles, size, _ = keys.shape
    return pl.pallas_call(
        functools.partial(prepare_kernel, scale, group),
        out_shape=[
            jax.ShapeDtypeStruct((tiles, width, size), BF16),
            jax.ShapeDtypeStruct((tiles, size, 2 * width), BF16),
            jax.ShapeDtypeStruct((halves * part + 8, width), F32),
        ],
        in_specs=[SMEM] + [ANY] * 5,
        out_specs=[VMEM] * 3,
        scratch_shapes=[pltpu.VMEM(a.shape, BF16) for a in (q, new_keys, new_values, keys, values)]
        + [pltpu.SemaphoreType.DMA] * 5,
        compiler_params=pltpu.CompilerParams(vmem_limit_bytes=44 << 20),
        cost_estimate=pl.CostEstimate(flops=1 << 24, bytes_accessed=16 << 20, transcendentals=1 << 15),
        name="prepare",
    )(lengths, q, new_keys, new_values, keys, values)


def attend_kernel(
    scale, halves, lengths, q_ref, k_ref, v_ref, o_ref, s_ref, m_ref, acc_ref, flag_ref, member, f_sem
):
    homes, held, width = q_ref.shape
    rows = held - META
    tiles, _, size = k_ref.shape
    part = rows // halves
    count = homes * halves

    for h in range(homes):
        flag_ref[h * halves : (h + 1) * halves, :] = q_ref[h, rows:, :].astype(F32)[:halves].astype(jnp.int32)
    f_copy = pltpu.make_async_copy(flag_ref, member, f_sem)
    f_copy.start()
    m_ref[...] = jnp.full(m_ref.shape, NEG, F32)
    acc_ref[...] = jnp.zeros(acc_ref.shape, F32)
    f_copy.wait()
    first = lax.axis_index("owner") * tiles

    def blocks(t):
        return [(slice(i * part, (i + 1) * part), member[i, first + t] > 0) for i in range(count)]

    def for_each_tile(body):
        @pl.loop(0, tiles)
        def _(t):
            used = member[0, first + t]
            for i in range(1, count):
                used = used + member[i, first + t]
            steps = jnp.where(used > 0, (lengths[t] + (STEP - 1)) // STEP, 0)
            for n in range(1, size // STEP + 1):

                @pl.when(steps == n)
                def _():
                    body(t, n * STEP)

    def score(t, wide):
        q = q_ref[:, :rows, :].reshape(homes * rows, width)
        s = jnp.dot(q, k_ref[t, :, :wide], preferred_element_type=F32)
        s_ref[t, :, :wide] = s
        for here, inside in blocks(t):
            x = s[here, :128]
            for j in range(128, wide, 128):
                x = jnp.maximum(x, s[here, j : j + 128])
            m_ref[here, :] = jnp.maximum(m_ref[here, :], jnp.where(inside, x, NEG))

    for_each_tile(score)
    peak = jnp.max(m_ref[...], axis=1, keepdims=True) * scale
    m_ref[...] = jnp.broadcast_to(peak, m_ref.shape)

    def weigh(t, wide):
        weights = []
        for here, inside in blocks(t):
            shift = jnp.where(inside, m_ref[here, :], -NEG)
            weights.append(
                jnp.concatenate(
                    [jnp.exp2(s_ref[t, here, j : j + 128] * scale - shift).astype(BF16) for j in range(0, wide, 128)],
                    axis=1,
                )
            )
        acc_ref[...] += jnp.dot(jnp.concatenate(weights, axis=0), v_ref[t, :wide, :], preferred_element_type=F32)

    for_each_tile(weigh)
    for h in range(homes):
        here = slice(h * rows, (h + 1) * rows)
        total = acc_ref[here, width:]
        o_ref[h, :rows, :] = (acc_ref[here, :width] / jnp.maximum(total, -1.0 / NEG)).astype(BF16)
        sums = jnp.concatenate(to_lanes(total, rows), axis=0)
        peaks = jnp.concatenate(to_lanes(m_ref[here, :], rows), axis=0)
        level = jnp.where(sums > 0.0, peaks + jnp.log(jnp.maximum(sums, -1.0 / NEG)) * LOG2, NEG)
        o_ref[h, rows:, :] = in_parts([level[b : b + 1] for b in range(rows // 128)])


def attend(q, keys, values, lengths, scale, halves):
    homes, held, width = q.shape
    tiles, _, size = keys.shape
    rows = held - META
    return pl.pallas_call(
        functools.partial(attend_kernel, scale, halves),
        out_shape=jax.ShapeDtypeStruct(q.shape, BF16),
        in_specs=[SMEM, VMEM, VMEM, VMEM],
        out_specs=VMEM,
        scratch_shapes=[
            pltpu.VMEM((tiles, homes * rows, size), F32),
            pltpu.VMEM((homes * rows, 128), F32),
            pltpu.VMEM((homes * rows, 2 * width), F32),
            pltpu.VMEM((homes * halves, 128), jnp.int32),
            pltpu.SMEM((homes * halves, 128), jnp.int32),
            pltpu.SemaphoreType.DMA,
        ],
        compiler_params=pltpu.CompilerParams(vmem_limit_bytes=44 << 20),
        cost_estimate=pl.CostEstimate(flops=1 << 30, bytes_accessed=1 << 20, transcendentals=1 << 18),
        name="attend",
    )(lengths, q, keys, values)


def weights_of(lines):
    level = jnp.concatenate(lines + [jnp.full((128 - len(lines), 128), 2 * NEG, F32)], axis=0)
    top = jnp.max(level, axis=0, keepdims=True)
    weight = jnp.exp2(level - top)
    total = jnp.sum(weight, axis=0, keepdims=True)
    return (weight / total).T, top + jnp.log(total) * LOG2


def merge_kernel(*refs):
    a_refs, o_refs = refs[:2], refs[2:]
    count = len(a_refs)
    homes, held, _ = a_refs[0].shape
    if len(o_refs) == 1:
        o_refs = [o_refs[0].at[h] for h in range(homes)]
    rows = held - META
    for h in range(homes):
        metas = [a[h, rows:, :].astype(F32) for a in a_refs]
        lines = []
        for b in range(rows // 128):
            weight, line = weights_of([levels(meta, b) for meta in metas])
            lines.append(line)
            here = slice(b * 128, (b + 1) * 128)
            acc = a_refs[0][h, here, :].astype(F32) * weight[:, 0:1]
            for i in range(1, count):
                acc = acc + a_refs[i][h, here, :].astype(F32) * weight[:, i : i + 1]
            o_refs[h][here, :] = acc.astype(BF16)
        o_refs[h][rows:, :] = in_parts(lines)


def merge(one, two, apart):
    homes, held, width = one.shape
    out = [jax.ShapeDtypeStruct((held, width), BF16)] * homes if apart else jax.ShapeDtypeStruct(one.shape, BF16)
    return pl.pallas_call(
        merge_kernel,
        out_shape=out,
        in_specs=[VMEM] * 2,
        out_specs=[VMEM] * homes if apart else VMEM,
        compiler_params=pltpu.CompilerParams(vmem_limit_bytes=16 << 20),
        cost_estimate=pl.CostEstimate(flops=1 << 34, bytes_accessed=4 << 20, transcendentals=1 << 14),
        name="merge",
    )(one, two)


def project_kernel(group, ranks, cores, *refs):
    a_refs, (own_ref, w_ref, keep_ref, give_ref, sum_ref, all_ref, flat_ref, held_ref, sems) = refs[:-9], refs[-9:]
    blocks, _, block = held_ref.shape
    copies = [
        pltpu.make_async_copy(w_ref.at[:, pl.ds(j * block, block)], held_ref.at[j], sems.at[j]) for j in range(blocks)
    ]
    for copy in copies:
        copy.start()
    rows, width = sum_ref.shape
    metas = [a[rows:, :].astype(F32) for a in a_refs]
    for b in range(rows // 128):
        weight, _ = weights_of([own_ref[rows + b : rows + b + 1, :]] + [levels(meta, b) for meta in metas])
        here = slice(b * 128, (b + 1) * 128)
        acc = own_ref[here, :] * weight[:, 0:1]
        for i, a in enumerate(a_refs):
            acc = acc + a[here, :].astype(F32) * weight[:, i + 1 : i + 2]
        sum_ref[here, :] = acc
    tokens = rows // group
    for g in range(group):
        all_ref[:, g * width : (g + 1) * width] = sum_ref[pl.ds(g, tokens, stride=group), :]
    chips = ranks // cores
    share = tokens // ranks
    rank = lax.axis_index("kvh")
    chip, core = rank // cores, rank % cores
    for i in range(cores):
        for d in range(chips):
            to = ((chip + d) % chips) * cores + (core + i) % cores
            at = (i * chips + d) * share
            flat_ref[at : at + share, :] = all_ref[pl.ds(pl.multiple_of(to * share, share), share), :]
    flat = flat_ref[...].astype(BF16)
    half = tokens // cores
    for j, copy in enumerate(copies):
        copy.wait()
        out = jnp.dot(flat, held_ref[j], preferred_element_type=F32).astype(BF16)
        keep_ref[:, j * block : (j + 1) * block] = out[:half]
        give_ref[:, j * block : (j + 1) * block] = out[half:]


def project(parts, own, weight, group, ranks, cores):
    held, width = parts[0].shape
    rows = held - META
    depth, columns = weight.shape
    tokens = rows // group
    block = 1024
    return pl.pallas_call(
        functools.partial(project_kernel, group, ranks, cores),
        out_shape=[jax.ShapeDtypeStruct((tokens // cores, columns), BF16)] * 2,
        in_specs=[VMEM] * (len(parts) + 1) + [ANY],
        out_specs=[VMEM] * 2,
        scratch_shapes=[
            pltpu.VMEM((rows, width), F32),
            pltpu.VMEM((tokens, depth), F32),
            pltpu.VMEM((tokens, depth), F32),
            pltpu.VMEM((columns // block, depth, block), BF16),
            pltpu.SemaphoreType.DMA((columns // block,)),
        ],
        compiler_params=pltpu.CompilerParams(vmem_limit_bytes=54 << 20),
        cost_estimate=pl.CostEstimate(flops=1 << 30, bytes_accessed=18 << 20, transcendentals=1 << 14),
        name="project",
    )(*parts, own, weight)


def local(
    queries, new_keys, new_values, ancestors, tile_keys, tile_values, tile_lengths, out_weight
):
    owners = lax.axis_size("owner")
    ranks = lax.axis_size("kvh")
    cores = 2
    chips = ranks // cores
    side = math.isqrt(owners)
    parts, new, group, width = queries.shape
    per_owner = tile_keys.shape[0]
    tiles = per_owner * owners
    scale = width**-0.5 * LOG2
    rows = parts * new * group

    def along(x, leg, step):
        pairs = []
        for o in range(owners):
            y, z = divmod(o, side)
            for k in range(ranks):
                if (k % cores + leg) % 2 == 0:
                    to = y * side + (z + step) % side
                else:
                    to = (y + step) % side * side + z
                pairs.append((o * ranks + k, to * ranks + k))
        return lax.ppermute(x, ("owner", "kvh"), pairs)

    member = jnp.any(ancestors[:, :, None] == jnp.arange(tiles, dtype=jnp.int32)[None, None, :], axis=1)
    meta = jnp.pad(member.astype(BF16), ((0, META - parts), (0, width - tiles)))
    home = jnp.concatenate([queries.reshape(rows, width), meta], axis=0)
    near = [along(home, 0, d) for d in range(1, side)]
    keys, values, own = prepare(
        tile_lengths,
        queries.reshape(parts, new * group, width),
        new_keys[:, :, 0],
        new_values[:, :, 0],
        tile_keys[:, 0],
        tile_values[:, 0],
        scale,
        group,
    )
    row, keys, values = lax.optimization_barrier((jnp.stack([home] + near), keys, values))
    order = sorted(range(side), key=lambda e: min(e, side - e))
    blocks = {e: along(row, 1, e) if e else row for e in order}
    back = []
    for e in order:
        block = blocks[e]
        if e:
            block, out = lax.optimization_barrier((block, out))
        out = attend(block, keys, values, tile_lengths, scale, parts)
        back.append(along(out, 1, -e) if e else out)
    merged = back[0]
    for i in range(1, side):
        merged = merge(merged, back[i], i == side - 1)
    final = [along(merged[d], 0, -d) if d else merged[d] for d in range(side)]
    keep, give = project(final, own, out_weight, group, ranks, cores)
    got = lax.ppermute(give, "kvh", [(k, k // cores * cores + (k + 1) % cores) for k in range(ranks)])
    both = keep.astype(F32) + got.astype(F32)
    share = both.shape[0] // chips
    result = both[:share]
    for d in range(1, chips):
        some = both[d * share : (d + 1) * share].astype(BF16)
        result = result + lax.ppermute(some, "kvh", [(k, (k + d * cores) % ranks) for k in range(ranks)]).astype(F32)
    return result.astype(BF16)


def solution(mesh):
    return jax.shard_map(
        local,
        mesh=mesh,
        in_specs=(
            P("owner", None, "kvh", None),
            P("owner", None, "kvh", None),
            P("owner", None, "kvh", None),
            P("owner", None),
            P("owner", "kvh", None, None),
            P("owner", "kvh", None, None),
            P("owner"),
            P("kvh", None),
        ),
        out_specs=P(("owner", "kvh"), None),
        check_vma=False,
    )
```

profile of v0, /device:TPU:1, one launch (start us, length us, event | category | flops | bytes accessed | tf_op | source)
XLA Modules:
  0.0 104.5 jit_solution(4622350298688100487)
XLA Ops:
  1.7 3.6 %collective-permute-start.2 = (bf16[528,128]{1,0:T(8,128)(2,1)S(1)}, bf16[528,128]{1,0:T(8,128)(2,1)S(1)}, u32[]{:S(2)}, u32[]{:S(2)}) collective-permute-start(bf16[528,128]{1,0:T(8,128)(2,1)S(1)} %get-tuple-element.41), channel_id=1, source_target_pairs={{0,24},{1,97},{2,26},{3,99},{4,28},{5,101},{6,30},{7,103},{8,0},{9... | collective-permute-start | bytes 405512 | tf_op jit(solution)/shard_map/ppermute | solution.py:327
  6.4 1.1 %copy-done = bf16[6,1,512,128]{3,2,1,0:T(8,128)(2,1)S(1)} copy-done((bf16[6,1,512,128]{3,2,1,0:T(8,128)(2,1)S(1)}, bf16[6,1,512,128]{3,2,1,0:T(8,128)(2,1)}, u32[]{:S(2)}) %copy-start) | copy-done | bytes 786456
  7.5 1.1 %copy-done.1 = bf16[6,1,512,128]{3,2,1,0:T(8,128)(2,1)S(1)} copy-done((bf16[6,1,512,128]{3,2,1,0:T(8,128)(2,1)S(1)}, bf16[6,1,512,128]{3,2,1,0:T(8,128)(2,1)}, u32[]{:S(2)}) %copy-start.1) | copy-done | bytes 786456
  11.7 2.4 %prepare.1 = (bf16[6,128,512]{2,1,0:T(8,128)(2,1)S(1)}, bf16[6,512,256]{2,1,0:T(8,128)(2,1)S(1)}, f32[520,128]{1,0:T(8,128)S(1)}) custom-call(s32[6]{0:T(128)S(1)} %copy-done.7, bf16[2,256,128]{2,1,0:T(8,128)(2,1)S(1)} %bitcast.14, bf16[2,32,128]{2,1,0:T(8,128)(2,1)S(1)} %bitcast.15, bf16[2,32,128]{2,1,0:T(8,128)(2,1)S(1)} %bitcast.16, ...), custom_call_target="tpu_custom_call" | custom-call | flops 16777216 | bytes 16777216 | tf_op jit(solution)/shard_map/prepare/pallas_call | solution.py:87
  14.2 1.7 %collective-permute-start.3 = (bf16[4,528,128]{2,1,0:T(8,128)(2,1)S(1)}, bf16[4,528,128]{2,1,0:T(8,128)(2,1)S(1)}, u32[]{:S(2)}, u32[]{:S(2)}) collective-permute-start(bf16[4,528,128]{2,1,0:T(8,128)(2,1)S(1)} %pad_maximum_fusion.q_ref), channel_id=1, source_target_pairs={{0,32},{1,9},{2,34},{3,11},{4,36},{5,13},{6,38},{7,15},{8,40},{9,1... | collective-permute-start | bytes 1622024 | tf_op jit(solution)/shard_map/ppermute | solution.py:327
  15.9 2.2 %collective-permute-start.5 = (bf16[4,528,128]{2,1,0:T(8,128)(2,1)S(1)}, bf16[4,528,128]{2,1,0:T(8,128)(2,1)S(1)}, u32[]{:S(2)}, u32[]{:S(2)}) collective-permute-start(bf16[4,528,128]{2,1,0:T(8,128)(2,1)S(1)} %pad_maximum_fusion.q_ref), channel_id=1, source_target_pairs={{0,96},{1,25},{2,98},{3,27},{4,100},{5,29},{6,102},{7,31},{8,104},... | collective-permute-start | bytes 1622024 | tf_op jit(solution)/shard_map/ppermute | solution.py:327
  18.1 1.2 %collective-permute-start.7 = (bf16[4,528,128]{2,1,0:T(8,128)(2,1)S(1)}, bf16[4,528,128]{2,1,0:T(8,128)(2,1)S(1)}, u32[]{:S(2)}, u32[]{:S(2)}) collective-permute-start(bf16[4,528,128]{2,1,0:T(8,128)(2,1)S(1)} %pad_maximum_fusion.q_ref), channel_id=1, source_target_pairs={{0,64},{1,17},{2,66},{3,19},{4,68},{5,21},{6,70},{7,23},{8,72},{9,... | collective-permute-start | bytes 1622024 | tf_op jit(solution)/shard_map/ppermute | solution.py:327
  19.4 8.2 %attend.4.refs_0_ = bf16[4,528,128]{2,1,0:T(8,128)(2,1)S(1)} custom-call(s32[6]{0:T(128)S(1)} %copy-done.7, bf16[4,528,128]{2,1,0:T(8,128)(2,1)S(1)} %pad_maximum_fusion.q_ref, bf16[6,128,512]{2,1,0:T(8,128)(2,1)S(1)} %get-tuple-element.23.k_ref, bf16[6,512,256]{2,1,0:T(8,128)(2,1)S(1)} %get-tuple-element.24.v_ref), custom_call_target="tpu_custom_call" | custom-call | flops 1073741824 | bytes 1048576 | tf_op jit(solution)/shard_map/attend/pallas_call | solution.py:179
  27.5 8.2 %attend.5 = bf16[4,528,128]{2,1,0:T(8,128)(2,1)S(1)} custom-call(s32[6]{0:T(128)S(1)} %copy-done.7, bf16[4,528,128]{2,1,0:T(8,128)(2,1)S(1)} %collective-permute-done.3.q_ref, bf16[6,128,512]{2,1,0:T(8,128)(2,1)S(1)} %get-tuple-element.23.k_ref, bf16[6,512,256]{2,1,0:T(8,128)(2,1)S(1)} %get-tuple-element.24.v_ref), custom_call_target="tpu_custom_call" | custom-call | flops 1073741824 | bytes 1048576 | tf_op jit(solution)/shard_map/attend/pallas_call | solution.py:179
  36.0 8.1 %attend.6 = bf16[4,528,128]{2,1,0:T(8,128)(2,1)S(1)} custom-call(s32[6]{0:T(128)S(1)} %copy-done.7, bf16[4,528,128]{2,1,0:T(8,128)(2,1)S(1)} %collective-permute-done.5.q_ref, bf16[6,128,512]{2,1,0:T(8,128)(2,1)S(1)} %get-tuple-element.23.k_ref, bf16[6,512,256]{2,1,0:T(8,128)(2,1)S(1)} %get-tuple-element.24.v_ref), custom_call_target="tpu_custom_call" | custom-call | flops 1073741824 | bytes 1048576 | tf_op jit(solution)/shard_map/attend/pallas_call | solution.py:179
  44.2 7.3 %attend.7 = bf16[4,528,128]{2,1,0:T(8,128)(2,1)S(1)} custom-call(s32[6]{0:T(128)S(1)} %copy-done.7, bf16[4,528,128]{2,1,0:T(8,128)(2,1)S(1)} %collective-permute-done.7.q_ref, bf16[6,128,512]{2,1,0:T(8,128)(2,1)S(1)} %get-tuple-element.23.k_ref, bf16[6,512,256]{2,1,0:T(8,128)(2,1)S(1)} %get-tuple-element.24.v_ref), custom_call_target="tpu_custom_call" | custom-call | flops 1073741824 | bytes 1048576 | tf_op jit(solution)/shard_map/attend/pallas_call | solution.py:179
  51.5 5.2 %collective-permute-start.8 = (bf16[4,528,128]{2,1,0:T(8,128)(2,1)S(1)}, bf16[4,528,128]{2,1,0:T(8,128)(2,1)S(1)}, u32[]{:S(2)}, u32[]{:S(2)}) collective-permute-start(bf16[4,528,128]{2,1,0:T(8,128)(2,1)S(1)} %attend.7), channel_id=1, source_target_pairs={{0,64},{1,17},{2,66},{3,19},{4,68},{5,21},{6,70},{7,23},{8,72},{9,... | collective-permute-start | bytes 1622024 | tf_op jit(solution)/shard_map/ppermute | solution.py:327
  58.7 5.0 %collective-permute-done.8.refs_1_ = bf16[4,528,128]{2,1,0:T(8,128)(2,1)S(1)} collective-permute-done((bf16[4,528,128]{2,1,0:T(8,128)(2,1)S(1)}, bf16[4,528,128]{2,1,0:T(8,128)(2,1)S(1)}, u32[]{:S(2)}, u32[]{:S(2)}) %collective-permute-start.8) | collective-permute-done | bytes 540704 | tf_op jit(solution)/shard_map/ppermute | solution.py:327
  65.4 1.5 %collective-permute-start.10 = (bf16[528,128]{1,0:T(8,128)(2,1)S(1)}, bf16[528,128]{1,0:T(8,128)(2,1)S(1)}, u32[]{:S(2)}, u32[]{:S(2)}) collective-permute-start(bf16[528,128]{1,0:T(8,128)(2,1)S(1)} %get-tuple-element.30), channel_id=1, source_target_pairs={{0,16},{1,65},{2,18},{3,67},{4,20},{5,69},{6,22},{7,71},{8,24},{9,... | collective-permute-start | bytes 405512 | tf_op jit(solution)/shard_map/ppermute | solution.py:327
  67.7 1.5 %collective-permute-done.9.refs_1_ = bf16[528,128]{1,0:T(8,128)(2,1)S(1)} collective-permute-done((bf16[528,128]{1,0:T(8,128)(2,1)S(1)}, bf16[528,128]{1,0:T(8,128)(2,1)S(1)}, u32[]{:S(2)}, u32[]{:S(2)}) %collective-permute-start.9) | collective-permute-done | bytes 135200 | tf_op jit(solution)/shard_map/ppermute | solution.py:327
  69.3 1.5 %collective-permute-done.10.refs_2_ = bf16[528,128]{1,0:T(8,128)(2,1)S(1)} collective-permute-done((bf16[528,128]{1,0:T(8,128)(2,1)S(1)}, bf16[528,128]{1,0:T(8,128)(2,1)S(1)}, u32[]{:S(2)}, u32[]{:S(2)}) %collective-permute-start.10) | collective-permute-done | bytes 135200 | tf_op jit(solution)/shard_map/ppermute | solution.py:327
  70.8 1.4 %collective-permute-done.11.refs_3_ = bf16[528,128]{1,0:T(8,128)(2,1)S(1)} collective-permute-done((bf16[528,128]{1,0:T(8,128)(2,1)S(1)}, bf16[528,128]{1,0:T(8,128)(2,1)S(1)}, u32[]{:S(2)}, u32[]{:S(2)}) %collective-permute-start.11) | collective-permute-done | bytes 135200 | tf_op jit(solution)/shard_map/ppermute | solution.py:327
  72.9 8.7 %project.1 = (bf16[32,8192]{1,0:T(8,128)(2,1)}, bf16[32,8192]{1,0:T(8,128)(2,1)}) custom-call(bf16[528,128]{1,0:T(8,128)(2,1)} %copy-done.4, bf16[528,128]{1,0:T(8,128)(2,1)} %copy-done.8, bf16[528,128]{1,0:T(8,128)(2,1)} %copy-done.9, bf16[528,128]{1,0:T(8,128)(2,1)} %copy-done.10, f32[520,128]{1,0:T(8,128)} %copy-done.3, bf16[1024,8192]{1,0:T(8,128)(2,1)} %refs_5_.1), custom_call_target="tpu_custom_call" | custom-call | flops 1073741824 | bytes 18874368 | tf_op jit(solution)/shard_map/project/pallas_call | solution.py:285
  81.5 7.0 %collective-permute-start.12 = (bf16[32,8192]{1,0:T(8,128)(2,1)}, bf16[32,8192]{1,0:T(8,128)(2,1)S(1)}, u32[]{:S(2)}, u32[]{:S(2)}) collective-permute-start(bf16[32,8192]{1,0:T(8,128)(2,1)} %get-tuple-element.34), channel_id=1, source_target_pairs={{0,1},{1,0},{2,3},{3,2},{4,5},{5,4},{6,7},{7,6},{8,9},{9,8},{10,11... | collective-permute-start | bytes 1572872 | tf_op jit(solution)/shard_map/ppermute | solution.py:358
  88.5 1.7 %collective-permute-done.12 = bf16[32,8192]{1,0:T(8,128)(2,1)S(1)} collective-permute-done((bf16[32,8192]{1,0:T(8,128)(2,1)}, bf16[32,8192]{1,0:T(8,128)(2,1)S(1)}, u32[]{:S(2)}, u32[]{:S(2)}) %collective-permute-start.12) | collective-permute-done | bytes 524320 | tf_op jit(solution)/shard_map/ppermute | solution.py:358
  90.3 1.2 %fusion.5 = (bf16[32,8192]{1,0:T(8,128)(2,1)S(1)}, f32[32,8192]{1,0:T(8,128)S(1)}) fusion(bf16[32,8192]{1,0:T(8,128)(2,1)S(1)} %collective-permute-done.12, bf16[32,8192]{1,0:T(8,128)(2,1)} %get-tuple-element.33), kind=kLoop, calls=%fused_computation.11 | loop fusion | flops 1048576 | bytes 2621440 | tf_op jit(solution)/shard_map/convert.4
  91.5 2.5 %collective-permute-start.15 = (bf16[8,8192]{1,0:T(8,128)(2,1)S(1)}, bf16[8,8192]{1,0:T(8,128)(2,1)S(1)}, u32[]{:S(2)}, u32[]{:S(2)}) collective-permute-start(bf16[8,8192]{1,0:T(8,128)(2,1)S(1)} %get-tuple-element.38), channel_id=1, source_target_pairs={{0,6},{1,7},{2,0},{3,1},{4,2},{5,3},{6,4},{7,5},{8,14},{9,15},{10,... | collective-permute-start | bytes 393224 | tf_op jit(solution)/shard_map/ppermute | solution.py:364
  95.1 4.1 %collective-permute-done.15 = bf16[8,8192]{1,0:T(8,128)(2,1)S(1)} collective-permute-done((bf16[8,8192]{1,0:T(8,128)(2,1)S(1)}, bf16[8,8192]{1,0:T(8,128)(2,1)S(1)}, u32[]{:S(2)}, u32[]{:S(2)}) %collective-permute-start.15) | collective-permute-done | bytes 131104 | tf_op jit(solution)/shard_map/ppermute | solution.py:364
  99.9 3.8 %collective-permute-done.13 = bf16[8,8192]{1,0:T(8,128)(2,1)S(1)} collective-permute-done((bf16[8,8192]{1,0:T(8,128)(2,1)S(1)}, bf16[8,8192]{1,0:T(8,128)(2,1)S(1)}, u32[]{:S(2)}, u32[]{:S(2)}) %collective-permute-start.13) | collective-permute-done | bytes 131104 | tf_op jit(solution)/shard_map/ppermute | solution.py:364
  (46 shorter events, 13.9 us)
Async XLA Ops:
  1.7 12.4 %collective-permute-start.2 = (bf16[528,128]{1,0:T(8,128)(2,1)S(1)}, bf16[528,128]{1,0:T(8,128)(2,1)S(1)}, u32[]{:S(2)}, u32[]{:S(2)}) collective-permute-start(bf16[528,128]{1,0:T(8,128)(2,1)S(1)} %get-tuple-element.41), channel_id=1, source_target_pairs={{0,24},{1,97},{2,26},{3,99},{4,28},{5,101},{6,30},{7,103},{8,0},{9... | collective-permute-start | bytes 405512 | tf_op jit(solution)/shard_map/ppermute | solution.py:327
  5.4 8.8 %collective-permute-start.1 = (bf16[528,128]{1,0:T(8,128)(2,1)S(1)}, bf16[528,128]{1,0:T(8,128)(2,1)S(1)}, u32[]{:S(2)}, u32[]{:S(2)}) collective-permute-start(bf16[528,128]{1,0:T(8,128)(2,1)S(1)} %get-tuple-element.41), channel_id=1, source_target_pairs={{0,16},{1,65},{2,18},{3,67},{4,20},{5,69},{6,22},{7,71},{8,24},{9,... | collective-permute-start | bytes 405512 | tf_op jit(solution)/shard_map/ppermute | solution.py:327
  5.7 8.4 %collective-permute-start = (bf16[528,128]{1,0:T(8,128)(2,1)S(1)}, bf16[528,128]{1,0:T(8,128)(2,1)S(1)}, u32[]{:S(2)}, u32[]{:S(2)}) collective-permute-start(bf16[528,128]{1,0:T(8,128)(2,1)S(1)} %get-tuple-element.41), channel_id=1, source_target_pairs={{0,8},{1,33},{2,10},{3,35},{4,12},{5,37},{6,14},{7,39},{8,16},{9,4... | collective-permute-start | bytes 405512 | tf_op jit(solution)/shard_map/ppermute | solution.py:327
  6.4 1.1 %copy-start = (bf16[6,1,512,128]{3,2,1,0:T(8,128)(2,1)S(1)}, bf16[6,1,512,128]{3,2,1,0:T(8,128)(2,1)}, u32[]{:S(2)}) copy-start(bf16[6,1,512,128]{3,2,1,0:T(8,128)(2,1)} %param.12) | copy-start | bytes 2359300
  7.5 1.1 %copy-start.1 = (bf16[6,1,512,128]{3,2,1,0:T(8,128)(2,1)S(1)}, bf16[6,1,512,128]{3,2,1,0:T(8,128)(2,1)}, u32[]{:S(2)}) copy-start(bf16[6,1,512,128]{3,2,1,0:T(8,128)(2,1)} %param.13) | copy-start | bytes 2359300
  8.7 0.9 copy-start.2
  9.6 0.7 copy-start.5
  10.3 0.7 copy-start.6
  14.1 43.6 %copy-start.3 = (f32[520,128]{1,0:T(8,128)}, f32[520,128]{1,0:T(8,128)S(1)}, u32[]{:S(2)}) copy-start(f32[520,128]{1,0:T(8,128)S(1)} %get-tuple-element.32.refs_4_) | copy-start | bytes 798724
  14.2 13.3 %collective-permute-start.3 = (bf16[4,528,128]{2,1,0:T(8,128)(2,1)S(1)}, bf16[4,528,128]{2,1,0:T(8,128)(2,1)S(1)}, u32[]{:S(2)}, u32[]{:S(2)}) collective-permute-start(bf16[4,528,128]{2,1,0:T(8,128)(2,1)S(1)} %pad_maximum_fusion.q_ref), channel_id=1, source_target_pairs={{0,32},{1,9},{2,34},{3,11},{4,36},{5,13},{6,38},{7,15},{8,40},{9,1... | collective-permute-start | bytes 1622024 | tf_op jit(solution)/shard_map/ppermute | solution.py:327
  15.9 20.0 %collective-permute-start.5 = (bf16[4,528,128]{2,1,0:T(8,128)(2,1)S(1)}, bf16[4,528,128]{2,1,0:T(8,128)(2,1)S(1)}, u32[]{:S(2)}, u32[]{:S(2)}) collective-permute-start(bf16[4,528,128]{2,1,0:T(8,128)(2,1)S(1)} %pad_maximum_fusion.q_ref), channel_id=1, source_target_pairs={{0,96},{1,25},{2,98},{3,27},{4,100},{5,29},{6,102},{7,31},{8,104},... | collective-permute-start | bytes 1622024 | tf_op jit(solution)/shard_map/ppermute | solution.py:327
  18.1 26.1 %collective-permute-start.7 = (bf16[4,528,128]{2,1,0:T(8,128)(2,1)S(1)}, bf16[4,528,128]{2,1,0:T(8,128)(2,1)S(1)}, u32[]{:S(2)}, u32[]{:S(2)}) collective-permute-start(bf16[4,528,128]{2,1,0:T(8,128)(2,1)S(1)} %pad_maximum_fusion.q_ref), channel_id=1, source_target_pairs={{0,64},{1,17},{2,66},{3,19},{4,68},{5,21},{6,70},{7,23},{8,72},{9,... | collective-permute-start | bytes 1622024 | tf_op jit(solution)/shard_map/ppermute | solution.py:327
  35.7 21.0 %collective-permute-start.4 = (bf16[4,528,128]{2,1,0:T(8,128)(2,1)S(1)}, bf16[4,528,128]{2,1,0:T(8,128)(2,1)S(1)}, u32[]{:S(2)}, u32[]{:S(2)}) collective-permute-start(bf16[4,528,128]{2,1,0:T(8,128)(2,1)S(1)} %attend.5), channel_id=1, source_target_pairs={{0,96},{1,25},{2,98},{3,27},{4,100},{5,29},{6,102},{7,31},{8,104},... | collective-permute-start | bytes 1622024 | tf_op jit(solution)/shard_map/ppermute | solution.py:327
  44.1 13.6 %collective-permute-start.6 = (bf16[4,528,128]{2,1,0:T(8,128)(2,1)S(1)}, bf16[4,528,128]{2,1,0:T(8,128)(2,1)S(1)}, u32[]{:S(2)}, u32[]{:S(2)}) collective-permute-start(bf16[4,528,128]{2,1,0:T(8,128)(2,1)S(1)} %attend.6), channel_id=1, source_target_pairs={{0,32},{1,9},{2,34},{3,11},{4,36},{5,13},{6,38},{7,15},{8,40},{9,1... | collective-permute-start | bytes 1622024 | tf_op jit(solution)/shard_map/ppermute | solution.py:327
  51.5 12.3 %collective-permute-start.8 = (bf16[4,528,128]{2,1,0:T(8,128)(2,1)S(1)}, bf16[4,528,128]{2,1,0:T(8,128)(2,1)S(1)}, u32[]{:S(2)}, u32[]{:S(2)}) collective-permute-start(bf16[4,528,128]{2,1,0:T(8,128)(2,1)S(1)} %attend.7), channel_id=1, source_target_pairs={{0,64},{1,17},{2,66},{3,19},{4,68},{5,21},{6,70},{7,23},{8,72},{9,... | collective-permute-start | bytes 1622024 | tf_op jit(solution)/shard_map/ppermute | solution.py:327
  65.4 3.9 %collective-permute-start.9 = (bf16[528,128]{1,0:T(8,128)(2,1)S(1)}, bf16[528,128]{1,0:T(8,128)(2,1)S(1)}, u32[]{:S(2)}, u32[]{:S(2)}) collective-permute-start(bf16[528,128]{1,0:T(8,128)(2,1)S(1)} %get-tuple-element.29), channel_id=1, source_target_pairs={{0,24},{1,97},{2,26},{3,99},{4,28},{5,101},{6,30},{7,103},{8,0},{9... | collective-permute-start | bytes 405512 | tf_op jit(solution)/shard_map/ppermute | solution.py:327
  65.4 5.4 %collective-permute-start.10 = (bf16[528,128]{1,0:T(8,128)(2,1)S(1)}, bf16[528,128]{1,0:T(8,128)(2,1)S(1)}, u32[]{:S(2)}, u32[]{:S(2)}) collective-permute-start(bf16[528,128]{1,0:T(8,128)(2,1)S(1)} %get-tuple-element.30), channel_id=1, source_target_pairs={{0,16},{1,65},{2,18},{3,67},{4,20},{5,69},{6,22},{7,71},{8,24},{9,... | collective-permute-start | bytes 405512 | tf_op jit(solution)/shard_map/ppermute | solution.py:327
  66.9 5.3 %collective-permute-start.11 = (bf16[528,128]{1,0:T(8,128)(2,1)S(1)}, bf16[528,128]{1,0:T(8,128)(2,1)S(1)}, u32[]{:S(2)}, u32[]{:S(2)}) collective-permute-start(bf16[528,128]{1,0:T(8,128)(2,1)S(1)} %get-tuple-element.31), channel_id=1, source_target_pairs={{0,8},{1,33},{2,10},{3,35},{4,12},{5,37},{6,14},{7,39},{8,16},{9,4... | collective-permute-start | bytes 405512 | tf_op jit(solution)/shard_map/ppermute | solution.py:327
  69.3 3.0 %copy-start.8 = (bf16[528,128]{1,0:T(8,128)(2,1)}, bf16[528,128]{1,0:T(8,128)(2,1)S(1)}, u32[]{:S(2)}) copy-start(bf16[528,128]{1,0:T(8,128)(2,1)S(1)} %collective-permute-done.9.refs_1_) | copy-start | bytes 405508
  70.8 1.4 %copy-start.9 = (bf16[528,128]{1,0:T(8,128)(2,1)}, bf16[528,128]{1,0:T(8,128)(2,1)S(1)}, u32[]{:S(2)}) copy-start(bf16[528,128]{1,0:T(8,128)(2,1)S(1)} %collective-permute-done.10.refs_2_) | copy-start | bytes 405508
  81.5 8.7 %collective-permute-start.12 = (bf16[32,8192]{1,0:T(8,128)(2,1)}, bf16[32,8192]{1,0:T(8,128)(2,1)S(1)}, u32[]{:S(2)}, u32[]{:S(2)}) collective-permute-start(bf16[32,8192]{1,0:T(8,128)(2,1)} %get-tuple-element.34), channel_id=1, source_target_pairs={{0,1},{1,0},{2,3},{3,2},{4,5},{5,4},{6,7},{7,6},{8,9},{9,8},{10,11... | collective-permute-start | bytes 1572872 | tf_op jit(solution)/shard_map/ppermute | solution.py:358
  91.5 7.7 %collective-permute-start.15 = (bf16[8,8192]{1,0:T(8,128)(2,1)S(1)}, bf16[8,8192]{1,0:T(8,128)(2,1)S(1)}, u32[]{:S(2)}, u32[]{:S(2)}) collective-permute-start(bf16[8,8192]{1,0:T(8,128)(2,1)S(1)} %get-tuple-element.38), channel_id=1, source_target_pairs={{0,6},{1,7},{2,0},{3,1},{4,2},{5,3},{6,4},{7,5},{8,14},{9,15},{10,... | collective-permute-start | bytes 393224 | tf_op jit(solution)/shard_map/ppermute | solution.py:364
  94.0 5.9 %collective-permute-start.14 = (bf16[8,8192]{1,0:T(8,128)(2,1)S(1)}, bf16[8,8192]{1,0:T(8,128)(2,1)S(1)}, u32[]{:S(2)}, u32[]{:S(2)}) collective-permute-start(bf16[8,8192]{1,0:T(8,128)(2,1)S(1)} %get-tuple-element.39), channel_id=1, source_target_pairs={{0,4},{1,5},{2,6},{3,7},{4,0},{5,1},{6,2},{7,3},{8,12},{9,13},{10,... | collective-permute-start | bytes 393224 | tf_op jit(solution)/shard_map/ppermute | solution.py:364
  94.5 9.2 %collective-permute-start.13 = (bf16[8,8192]{1,0:T(8,128)(2,1)S(1)}, bf16[8,8192]{1,0:T(8,128)(2,1)S(1)}, u32[]{:S(2)}, u32[]{:S(2)}) collective-permute-start(bf16[8,8192]{1,0:T(8,128)(2,1)S(1)} %get-tuple-element.37), channel_id=1, source_target_pairs={{0,2},{1,3},{2,4},{3,5},{4,6},{5,7},{6,0},{7,1},{8,10},{9,11},{10,... | collective-permute-start | bytes 393224 | tf_op jit(solution)/shard_map/ppermute | solution.py:364
  (3 other events, 2.0 us)
where the time goes:
time: 104 us
  Pallas kernels  45.8 us (44%)
  starting transfers between devices  28.3 us (27%)
  waiting for transfers between devices  19.9 us (19%)
  local copies, waits for them, and re-layouts  6.59 us (6%)
  other arithmetic  3.67 us (4%)
    pallas_call x4, Pallas kernels, attend(): pl.pallas_call(functools.partial(attend_kernel, scale, halves), out_shape...  31.7 us
    ppermute x12, starting transfers between devices, along(): return lax.ppermute(x, ('owner', 'kvh'), pairs)  17.7 us
    ppermute x12, waiting for transfers between devices, along(): return lax.ppermute(x, ('owner', 'kvh'), pairs)  9.5 us
    pallas_call x1, Pallas kernels, project(): pl.pallas_call(functools.partial(project_kernel, group, ranks, cores), ou...  8.66 us
    ppermute x3, waiting for transfers between devices, local(): lax.ppermute(some, 'kvh', [(k, (k + d * cores) % ranks) for k in range(ra...  8.62 us
    ppermute x1, starting transfers between devices, local(): lax.ppermute(give, 'kvh', [(k, k // cores * cores + (k + 1) % cores) for...  6.97 us
    unnamed x22, local copies, waits for them, and re-layouts  6.56 us
    ppermute x3, starting transfers between devices, local(): lax.ppermute(some, 'kvh', [(k, (k + d * cores) % ranks) for k in range(ra...  3.66 us
  transfers between devices with their start and end apart: 16, of which 8 were waited for; matrix products, arithmetic and copies ran while one was open for 0% of the time, Pallas kernels for 35%

commit v1 on v0

--- a/solution.py
+++ b/solution.py
@@ -98,7 +98,7 @@
         compiler_params=pltpu.CompilerParams(vmem_limit_bytes=44 << 20),
         cost_estimate=pl.CostEstimate(flops=1 << 24, bytes_accessed=16 << 20, transcendentals=1 << 15),
         name="prepare",
-    )(lengths, q, new_keys, new_values, keys, values)
+    )(lengths, *(pltpu.with_memory_space_constraint(a, pltpu.HBM) for a in (q, new_keys, new_values, keys, values)))
 
 
 def attend_kernel(
@@ -110,28 +110,34 @@
     part = rows // halves
     count = homes * halves
 
-    for h in range(homes):
-        flag_ref[h * halves : (h + 1) * halves, :] = q_ref[h, rows:, :].astype(F32)[:halves].astype(jnp.int32)
+    names = jnp.concatenate([q_ref[h, rows:, :].astype(F32)[:halves] for h in range(homes)], axis=0)
+    lane = lax.broadcasted_iota(jnp.int32, names.shape, 1)
+    first = (lax.axis_index("owner") * tiles).astype(F32)
+    flags = jnp.zeros(names.shape, F32)
+    for t in range(tiles):
+        inside = jnp.max(jnp.where(names == first + t, 1.0, 0.0), axis=1, keepdims=True)
+        flags = jnp.where(lane == t, inside, flags)
+    flag_ref[:count, :] = flags.astype(jnp.int32)
+    flag_ref[count:, :] = jnp.broadcast_to(jnp.sum(flags, axis=0, keepdims=True), names.shape).astype(jnp.int32)
     f_copy = pltpu.make_async_copy(flag_ref, member, f_sem)
     f_copy.start()
     m_ref[...] = jnp.full(m_ref.shape, NEG, F32)
     acc_ref[...] = jnp.zeros(acc_ref.shape, F32)
     f_copy.wait()
-    first = lax.axis_index("owner") * tiles
 
     def blocks(t):
-        return [(slice(i * part, (i + 1) * part), member[i, first + t] > 0) for i in range(count)]
+        return [(slice(i * part, (i + 1) * part), member[i, t] > 0) for i in range(count)]
 
     def for_each_tile(body):
         @pl.loop(0, tiles)
         def _(t):
-            used = member[0, first + t]
-            for i in range(1, count):
-                used = used + member[i, first + t]
-            steps = jnp.where(used > 0, (lengths[t] + (STEP - 1)) // STEP, 0)
+            used = member[count, t] > 0
             for n in range(1, size // STEP + 1):
-
-                @pl.when(steps == n)
+                fits = lengths[t] > (n - 1) * STEP
+                if n * STEP < size:
+                    fits = fits & (lengths[t] <= n * STEP)
+
+                @pl.when(used & fits)
                 def _():
                     body(t, n * STEP)
 
@@ -185,8 +191,8 @@
             pltpu.VMEM((tiles, homes * rows, size), F32),
             pltpu.VMEM((homes * rows, 128), F32),
             pltpu.VMEM((homes * rows, 2 * width), F32),
-            pltpu.VMEM((homes * halves, 128), jnp.int32),
-            pltpu.SMEM((homes * halves, 128), jnp.int32),
+            pltpu.VMEM((2 * homes * halves, 128), jnp.int32),
+            pltpu.SMEM((2 * homes * halves, 128), jnp.int32),
             pltpu.SemaphoreType.DMA,
         ],
         compiler_params=pltpu.CompilerParams(vmem_limit_bytes=44 << 20),
@@ -294,7 +300,7 @@
             pltpu.VMEM((columns // block, depth, block), BF16),
             pltpu.SemaphoreType.DMA((columns // block,)),
         ],
-        compiler_params=pltpu.CompilerParams(vmem_limit_bytes=54 << 20),
+        compiler_params=pltpu.CompilerParams(vmem_limit_bytes=50 << 20),
         cost_estimate=pl.CostEstimate(flops=1 << 30, bytes_accessed=18 << 20, transcendentals=1 << 14),
         name="project",
     )(*parts, own, weight)
@@ -310,7 +316,6 @@
     side = math.isqrt(owners)
     parts, new, group, width = queries.shape
     per_owner = tile_keys.shape[0]
-    tiles = per_owner * owners
     scale = width**-0.5 * LOG2
     rows = parts * new * group
 
@@ -326,9 +331,8 @@
                 pairs.append((o * ranks + k, to * ranks + k))
         return lax.ppermute(x, ("owner", "kvh"), pairs)
 
-    member = jnp.any(ancestors[:, :, None] == jnp.arange(tiles, dtype=jnp.int32)[None, None, :], axis=1)
-    meta = jnp.pad(member.astype(BF16), ((0, META - parts), (0, width - tiles)))
-    home = jnp.concatenate([queries.reshape(rows, width), meta], axis=0)
+    names = jnp.pad(ancestors.astype(BF16), ((0, META - parts), (0, width - ancestors.shape[1])), constant_values=-1)
+    home = jnp.concatenate([queries.reshape(rows, width), names], axis=0)
     near = [along(home, 0, d) for d in range(1, side)]
     keys, values, own = prepare(
         tile_lengths,
@@ -342,9 +346,12 @@
     )
     row, keys, values = lax.optimization_barrier((jnp.stack([home] + near), keys, values))
     order = sorted(range(side), key=lambda e: min(e, side - e))
-    blocks = {e: along(row, 1, e) if e else row for e in order}
+    blocks = {e: along(row, 1, e) if e else row for e in order[:-1]}
     back = []
     for e in order:
+        if e == order[1]:
+            late, out = lax.optimization_barrier((row, out))
+            blocks[order[-1]] = along(late, 1, order[-1])
         block = blocks[e]
         if e:
             block, out = lax.optimization_barrier((block, out))
@@ -356,12 +363,14 @@
     final = [along(merged[d], 0, -d) if d else merged[d] for d in range(side)]
     keep, give = project(final, own, out_weight, group, ranks, cores)
     got = lax.ppermute(give, "kvh", [(k, k // cores * cores + (k + 1) % cores) for k in range(ranks)])
-    both = keep.astype(F32) + got.astype(F32)
-    share = both.shape[0] // chips
-    result = both[:share]
-    for d in range(1, chips):
-        some = both[d * share : (d + 1) * share].astype(BF16)
-        result = result + lax.ppermute(some, "kvh", [(k, (k + d * cores) % ranks) for k in range(ranks)]).astype(F32)
+    share = keep.shape[0] // chips
+    pieces = [
+        keep[d * share : (d + 1) * share].astype(F32) + got[d * share : (d + 1) * share].astype(F32) for d in range(chips)
+    ]
+    result = pieces[0]
+    for d in sorted(range(1, chips), key=lambda d: min(d, chips - d)):
+        pairs = [(k, (k + d * cores) % ranks) for k in range(ranks)]
+        result = result + lax.ppermute(pieces[d].astype(BF16), "kvh", pairs).astype(F32)
     return result.astype(BF16)
 
 

time: 104 us -> 94.4 us (0.908)
  Pallas kernels: 45.8 us -> 39.3 us
  local copies, waits for them, and re-layouts: 6.59 us -> 0.65 us
  starting transfers between devices: 28.3 us -> 33.3 us
  other arithmetic: 3.67 us -> 2.53 us
    pallas_call x4, Pallas kernels: 31.7 us -> 25.7 us  [attend(): pl.pallas_call(functools.partial(attend_kernel, scale, halves), out_shape...]
    unnamed x22 -> x2, local copies, waits for them, and re-layouts: 6.56 us -> 0.65 us
    ppermute x3, waiting for transfers between devices: 8.62 us -> 4.91 us  [local(): lax.ppermute(pieces[d].astype(BF16), 'kvh', pairs).astype(F32)]
    ppermute x12, waiting for transfers between devices: 9.5 us -> 12.7 us  [along(): return lax.ppermute(x, ('owner', 'kvh'), pairs)]
    ppermute x12, starting transfers between devices: 17.7 us -> 19.6 us  [along(): return lax.ppermute(x, ('owner', 'kvh'), pairs)]
    ppermute x1, starting transfers between devices: 6.97 us -> 8.79 us  [local(): lax.ppermute(give, 'kvh', [(k, k // cores * cores + (k + 1) % cores) for...]
    pallas_call x1, Pallas kernels: 8.66 us -> 7.03 us  [project(): pl.pallas_call(functools.partial(project_kernel, group, ranks, cores), ou...]
    ppermute x3, starting transfers between devices: 3.66 us -> 4.89 us  [local(): lax.ppermute(pieces[d].astype(BF16), 'kvh', pairs).astype(F32)]
  transfers between devices with their start and end apart: 16 -> 16, of which waited for: 8 -> 9; matrix products, arithmetic and copies ran while one was open for 0% -> 0% of each run, Pallas kernels for 35% -> 33%
where the time goes in v1:
time: 94.4 us; the launch traced here: 95.1 us
  Pallas kernels  39.3 us (42%)
  starting transfers between devices  33.3 us (35%)
  waiting for transfers between devices  19.2 us (20%)
  other arithmetic  2.53 us (3%)
    pallas_call x4, Pallas kernels, attend(): pl.pallas_call(functools.partial(attend_kernel, scale, halves), out_shape...  25.7 us
    ppermute x12, starting transfers between devices, along(): return lax.ppermute(x, ('owner', 'kvh'), pairs)  19.6 us
    ppermute x12, waiting for transfers between devices, along(): return lax.ppermute(x, ('owner', 'kvh'), pairs)  12.7 us
    ppermute x1, starting transfers between devices, local(): lax.ppermute(give, 'kvh', [(k, k // cores * cores + (k + 1) % cores) for...  8.79 us
    pallas_call x1, Pallas kernels, project(): pl.pallas_call(functools.partial(project_kernel, group, ranks, cores), ou...  7.03 us
    ppermute x3, waiting for transfers between devices, local(): lax.ppermute(pieces[d].astype(BF16), 'kvh', pairs).astype(F32)  4.91 us
    ppermute x3, starting transfers between devices, local(): lax.ppermute(pieces[d].astype(BF16), 'kvh', pairs).astype(F32)  4.89 us
    pallas_call x1, Pallas kernels, prepare(): pl.pallas_call(functools.partial(prepare_kernel, scale, group), out_shape...  3.6 us
  transfers between devices with their start and end apart: 16, of which 9 were waited for; matrix products, arithmetic and copies ran while one was open for 0% of the time, Pallas kernels for 33%

profile of v1, /device:TPU:1, one launch (start us, length us, event | category | flops | bytes accessed | tf_op | source)
XLA Modules:
  0.0 95.1 jit_solution(10721924521154612591)
XLA Ops:
  1.6 3.8 %collective-permute-start.1 = (bf16[528,128]{1,0:T(8,128)(2,1)S(1)}, bf16[528,128]{1,0:T(8,128)(2,1)S(1)}, u32[]{:S(2)}, u32[]{:S(2)}) collective-permute-start(bf16[528,128]{1,0:T(8,128)(2,1)S(1)} %get-tuple-element.39), channel_id=1, source_target_pairs={{0,16},{1,65},{2,18},{3,67},{4,20},{5,69},{6,22},{7,71},{8,24},{9,... | collective-permute-start | bytes 405512 | tf_op jit(solution)/shard_map/ppermute | solution.py:332
  5.8 2.3 %collective-permute-start.2 = (bf16[528,128]{1,0:T(8,128)(2,1)S(1)}, bf16[528,128]{1,0:T(8,128)(2,1)S(1)}, u32[]{:S(2)}, u32[]{:S(2)}) collective-permute-start(bf16[528,128]{1,0:T(8,128)(2,1)S(1)} %get-tuple-element.39), channel_id=1, source_target_pairs={{0,24},{1,97},{2,26},{3,99},{4,28},{5,101},{6,30},{7,103},{8,0},{9... | collective-permute-start | bytes 405512 | tf_op jit(solution)/shard_map/ppermute | solution.py:332
  8.8 3.6 %prepare.1 = (bf16[6,128,512]{2,1,0:T(8,128)(2,1)S(1)}, bf16[6,512,256]{2,1,0:T(8,128)(2,1)S(1)}, f32[520,128]{1,0:T(8,128)S(1)}) custom-call(s32[6]{0:T(128)S(1)} %copy-done, bf16[2,256,128]{2,1,0:T(8,128)(2,1)} %bitcast.14, bf16[2,32,128]{2,1,0:T(8,128)(2,1)} %bitcast.18, bf16[2,32,128]{2,1,0:T(8,128)(2,1)} %bitcast.19, bf16[6,512,128]{2,1,0:T(8,128)(2,1)} %bitcast.11, ...), custom_call_target="tpu_custom_call" | custom-call | flops 16777216 | bytes 16777216 | tf_op jit(solution)/shard_map/prepare/pallas_call | solution.py:87
  12.5 1.7 %collective-permute-start.3 = (bf16[4,528,128]{2,1,0:T(8,128)(2,1)S(1)}, bf16[4,528,128]{2,1,0:T(8,128)(2,1)S(1)}, u32[]{:S(2)}, u32[]{:S(2)}) collective-permute-start(bf16[4,528,128]{2,1,0:T(8,128)(2,1)S(1)} %pad_maximum_fusion.q_ref), channel_id=1, source_target_pairs={{0,32},{1,9},{2,34},{3,11},{4,36},{5,13},{6,38},{7,15},{8,40},{9,1... | collective-permute-start | bytes 1622024 | tf_op jit(solution)/shard_map/ppermute | solution.py:332
  14.2 2.2 %collective-permute-start.5 = (bf16[4,528,128]{2,1,0:T(8,128)(2,1)S(1)}, bf16[4,528,128]{2,1,0:T(8,128)(2,1)S(1)}, u32[]{:S(2)}, u32[]{:S(2)}) collective-permute-start(bf16[4,528,128]{2,1,0:T(8,128)(2,1)S(1)} %pad_maximum_fusion.q_ref), channel_id=1, source_target_pairs={{0,96},{1,25},{2,98},{3,27},{4,100},{5,29},{6,102},{7,31},{8,104},... | collective-permute-start | bytes 1622024 | tf_op jit(solution)/shard_map/ppermute | solution.py:332
  16.4 5.7 %attend.4.refs_0_ = bf16[4,528,128]{2,1,0:T(8,128)(2,1)S(1)} custom-call(s32[6]{0:T(128)S(1)} %copy-done, bf16[4,528,128]{2,1,0:T(8,128)(2,1)S(1)} %pad_maximum_fusion.q_ref, bf16[6,128,512]{2,1,0:T(8,128)(2,1)S(1)} %get-tuple-element.23.k_ref, bf16[6,512,256]{2,1,0:T(8,128)(2,1)S(1)} %get-tuple-element.24.v_ref), custom_call_target="tpu_custom_call" | custom-call | flops 1073741824 | bytes 1048576 | tf_op jit(solution)/shard_map/attend/pallas_call | solution.py:185
  23.4 7.2 %attend.5 = bf16[4,528,128]{2,1,0:T(8,128)(2,1)S(1)} custom-call(s32[6]{0:T(128)S(1)} %copy-done, bf16[4,528,128]{2,1,0:T(8,128)(2,1)S(1)} %collective-permute-done.3.q_ref, bf16[6,128,512]{2,1,0:T(8,128)(2,1)S(1)} %get-tuple-element.23.k_ref, bf16[6,512,256]{2,1,0:T(8,128)(2,1)S(1)} %get-tuple-element.24.v_ref), custom_call_target="tpu_custom_call" | custom-call | flops 1073741824 | bytes 1048576 | tf_op jit(solution)/shard_map/attend/pallas_call | solution.py:185
  30.6 2.3 %collective-permute-start.4 = (bf16[4,528,128]{2,1,0:T(8,128)(2,1)S(1)}, bf16[4,528,128]{2,1,0:T(8,128)(2,1)S(1)}, u32[]{:S(2)}, u32[]{:S(2)}) collective-permute-start(bf16[4,528,128]{2,1,0:T(8,128)(2,1)S(1)} %attend.5), channel_id=1, source_target_pairs={{0,96},{1,25},{2,98},{3,27},{4,100},{5,29},{6,102},{7,31},{8,104},... | collective-permute-start | bytes 1622024 | tf_op jit(solution)/shard_map/ppermute | solution.py:332
  32.8 7.2 %attend.6 = bf16[4,528,128]{2,1,0:T(8,128)(2,1)S(1)} custom-call(s32[6]{0:T(128)S(1)} %copy-done, bf16[4,528,128]{2,1,0:T(8,128)(2,1)S(1)} %collective-permute-done.5.q_ref, bf16[6,128,512]{2,1,0:T(8,128)(2,1)S(1)} %get-tuple-element.23.k_ref, bf16[6,512,256]{2,1,0:T(8,128)(2,1)S(1)} %get-tuple-element.24.v_ref), custom_call_target="tpu_custom_call" | custom-call | flops 1073741824 | bytes 1048576 | tf_op jit(solution)/shard_map/attend/pallas_call | solution.py:185
  40.1 5.7 %attend.7 = bf16[4,528,128]{2,1,0:T(8,128)(2,1)S(1)} custom-call(s32[6]{0:T(128)S(1)} %copy-done, bf16[4,528,128]{2,1,0:T(8,128)(2,1)S(1)} %collective-permute-done.7.q_ref, bf16[6,128,512]{2,1,0:T(8,128)(2,1)S(1)} %get-tuple-element.23.k_ref, bf16[6,512,256]{2,1,0:T(8,128)(2,1)S(1)} %get-tuple-element.24.v_ref), custom_call_target="tpu_custom_call" | custom-call | flops 1073741824 | bytes 1048576 | tf_op jit(solution)/shard_map/attend/pallas_call | solution.py:185
  45.8 1.6 %collective-permute-start.8 = (bf16[4,528,128]{2,1,0:T(8,128)(2,1)S(1)}, bf16[4,528,128]{2,1,0:T(8,128)(2,1)S(1)}, u32[]{:S(2)}, u32[]{:S(2)}) collective-permute-start(bf16[4,528,128]{2,1,0:T(8,128)(2,1)S(1)} %attend.7), channel_id=1, source_target_pairs={{0,64},{1,17},{2,66},{3,19},{4,68},{5,21},{6,70},{7,23},{8,72},{9,... | collective-permute-start | bytes 1622024 | tf_op jit(solution)/shard_map/ppermute | solution.py:332
  48.3 1.4 %collective-permute-done.6.refs_1_ = bf16[4,528,128]{2,1,0:T(8,128)(2,1)S(1)} collective-permute-done((bf16[4,528,128]{2,1,0:T(8,128)(2,1)S(1)}, bf16[4,528,128]{2,1,0:T(8,128)(2,1)S(1)}, u32[]{:S(2)}, u32[]{:S(2)}) %collective-permute-start.6) | collective-permute-done | bytes 540704 | tf_op jit(solution)/shard_map/ppermute | solution.py:332
  50.8 5.1 %collective-permute-done.8.refs_1_ = bf16[4,528,128]{2,1,0:T(8,128)(2,1)S(1)} collective-permute-done((bf16[4,528,128]{2,1,0:T(8,128)(2,1)S(1)}, bf16[4,528,128]{2,1,0:T(8,128)(2,1)S(1)}, u32[]{:S(2)}, u32[]{:S(2)}) %collective-permute-start.8) | collective-permute-done | bytes 540704 | tf_op jit(solution)/shard_map/ppermute | solution.py:332
  56.9 3.4 %collective-permute-start.9 = (bf16[528,128]{1,0:T(8,128)(2,1)S(1)}, bf16[528,128]{1,0:T(8,128)(2,1)S(1)}, u32[]{:S(2)}, u32[]{:S(2)}) collective-permute-start(bf16[528,128]{1,0:T(8,128)(2,1)S(1)} %get-tuple-element.29), channel_id=1, source_target_pairs={{0,24},{1,97},{2,26},{3,99},{4,28},{5,101},{6,30},{7,103},{8,0},{9... | collective-permute-start | bytes 405512 | tf_op jit(solution)/shard_map/ppermute | solution.py:332
  61.2 2.5 %collective-permute-done.9.refs_1_ = bf16[528,128]{1,0:T(8,128)(2,1)S(1)} collective-permute-done((bf16[528,128]{1,0:T(8,128)(2,1)S(1)}, bf16[528,128]{1,0:T(8,128)(2,1)S(1)}, u32[]{:S(2)}, u32[]{:S(2)}) %collective-permute-start.9) | collective-permute-done | bytes 135200 | tf_op jit(solution)/shard_map/ppermute | solution.py:332
  63.7 2.1 %collective-permute-done.10.refs_2_ = bf16[528,128]{1,0:T(8,128)(2,1)S(1)} collective-permute-done((bf16[528,128]{1,0:T(8,128)(2,1)S(1)}, bf16[528,128]{1,0:T(8,128)(2,1)S(1)}, u32[]{:S(2)}, u32[]{:S(2)}) %collective-permute-start.10) | collective-permute-done | bytes 135200 | tf_op jit(solution)/shard_map/ppermute | solution.py:332
  65.7 1.4 %collective-permute-done.11.refs_3_ = bf16[528,128]{1,0:T(8,128)(2,1)S(1)} collective-permute-done((bf16[528,128]{1,0:T(8,128)(2,1)S(1)}, bf16[528,128]{1,0:T(8,128)(2,1)S(1)}, u32[]{:S(2)}, u32[]{:S(2)}) %collective-permute-start.11) | collective-permute-done | bytes 135200 | tf_op jit(solution)/shard_map/ppermute | solution.py:332
  67.1 7.0 %project.1 = (bf16[32,8192]{1,0:T(8,128)(2,1)S(1)}, bf16[32,8192]{1,0:T(8,128)(2,1)S(1)}) custom-call(bf16[528,128]{1,0:T(8,128)(2,1)S(1)} %get-tuple-element.28.refs_0_, bf16[528,128]{1,0:T(8,128)(2,1)S(1)} %collective-permute-done.9.refs_1_, bf16[528,128]{1,0:T(8,128)(2,1)S(1)} %collective-permute-done.10.refs_2_, ...), custom_call_target="tpu_custom_call" | custom-call | flops 1073741824 | bytes 18874368 | tf_op jit(solution)/shard_map/project/pallas_call | solution.py:291
  74.1 8.8 %collective-permute-start.12 = (bf16[32,8192]{1,0:T(8,128)(2,1)S(1)}, bf16[32,8192]{1,0:T(8,128)(2,1)S(1)}, u32[]{:S(2)}, u32[]{:S(2)}) collective-permute-start(bf16[32,8192]{1,0:T(8,128)(2,1)S(1)} %get-tuple-element.34), channel_id=1, source_target_pairs={{0,1},{1,0},{2,3},{3,2},{4,5},{5,4},{6,7},{7,6},{8,9},{9,8},{10,11... | collective-permute-start | bytes 1572872 | tf_op jit(solution)/shard_map/ppermute | solution.py:365
  82.9 1.5 %collective-permute-done.12 = bf16[32,8192]{1,0:T(8,128)(2,1)S(1)} collective-permute-done((bf16[32,8192]{1,0:T(8,128)(2,1)S(1)}, bf16[32,8192]{1,0:T(8,128)(2,1)S(1)}, u32[]{:S(2)}, u32[]{:S(2)}) %collective-permute-start.12) | collective-permute-done | bytes 524320 | tf_op jit(solution)/shard_map/ppermute | solution.py:365
  84.6 1.3 %collective-permute-start.13 = (bf16[8,8192]{1,0:T(8,128)(2,1)S(1)}, bf16[8,8192]{1,0:T(8,128)(2,1)S(1)}, u32[]{:S(2)}, u32[]{:S(2)}) collective-permute-start(bf16[8,8192]{1,0:T(8,128)(2,1)S(1)} %get-tuple-element.35), channel_id=1, source_target_pairs={{0,2},{1,3},{2,4},{3,5},{4,6},{5,7},{6,0},{7,1},{8,10},{9,11},{10,... | collective-permute-start | bytes 393224 | tf_op jit(solution)/shard_map/ppermute | solution.py:373
  85.9 2.4 %collective-permute-start.15 = (bf16[8,8192]{1,0:T(8,128)(2,1)S(1)}, bf16[8,8192]{1,0:T(8,128)(2,1)S(1)}, u32[]{:S(2)}, u32[]{:S(2)}) collective-permute-start(bf16[8,8192]{1,0:T(8,128)(2,1)S(1)} %get-tuple-element.36), channel_id=1, source_target_pairs={{0,4},{1,5},{2,6},{3,7},{4,0},{5,1},{6,2},{7,3},{8,12},{9,13},{10,... | collective-permute-start | bytes 393224 | tf_op jit(solution)/shard_map/ppermute | solution.py:373
  88.3 1.1 %collective-permute-start.14 = (bf16[8,8192]{1,0:T(8,128)(2,1)S(1)}, bf16[8,8192]{1,0:T(8,128)(2,1)S(1)}, u32[]{:S(2)}, u32[]{:S(2)}) collective-permute-start(bf16[8,8192]{1,0:T(8,128)(2,1)S(1)} %get-tuple-element.37), channel_id=1, source_target_pairs={{0,6},{1,7},{2,0},{3,1},{4,2},{5,3},{6,4},{7,5},{8,14},{9,15},{10,... | collective-permute-start | bytes 393224 | tf_op jit(solution)/shard_map/ppermute | solution.py:373
  90.5 3.8 %collective-permute-done.15 = bf16[8,8192]{1,0:T(8,128)(2,1)S(1)} collective-permute-done((bf16[8,8192]{1,0:T(8,128)(2,1)S(1)}, bf16[8,8192]{1,0:T(8,128)(2,1)S(1)}, u32[]{:S(2)}, u32[]{:S(2)}) %collective-permute-start.15) | collective-permute-done | bytes 131104 | tf_op jit(solution)/shard_map/ppermute | solution.py:373
  (24 shorter events, 9.9 us)
Async XLA Ops:
  1.6 10.8 %collective-permute-start.1 = (bf16[528,128]{1,0:T(8,128)(2,1)S(1)}, bf16[528,128]{1,0:T(8,128)(2,1)S(1)}, u32[]{:S(2)}, u32[]{:S(2)}) collective-permute-start(bf16[528,128]{1,0:T(8,128)(2,1)S(1)} %get-tuple-element.39), channel_id=1, source_target_pairs={{0,16},{1,65},{2,18},{3,67},{4,20},{5,69},{6,22},{7,71},{8,24},{9,... | collective-permute-start | bytes 405512 | tf_op jit(solution)/shard_map/ppermute | solution.py:332
  5.4 7.0 %collective-permute-start = (bf16[528,128]{1,0:T(8,128)(2,1)S(1)}, bf16[528,128]{1,0:T(8,128)(2,1)S(1)}, u32[]{:S(2)}, u32[]{:S(2)}) collective-permute-start(bf16[528,128]{1,0:T(8,128)(2,1)S(1)} %get-tuple-element.39), channel_id=1, source_target_pairs={{0,8},{1,33},{2,10},{3,35},{4,12},{5,37},{6,14},{7,39},{8,16},{9,4... | collective-permute-start | bytes 405512 | tf_op jit(solution)/shard_map/ppermute | solution.py:332
  5.8 6.6 %collective-permute-start.2 = (bf16[528,128]{1,0:T(8,128)(2,1)S(1)}, bf16[528,128]{1,0:T(8,128)(2,1)S(1)}, u32[]{:S(2)}, u32[]{:S(2)}) collective-permute-start(bf16[528,128]{1,0:T(8,128)(2,1)S(1)} %get-tuple-element.39), channel_id=1, source_target_pairs={{0,24},{1,97},{2,26},{3,99},{4,28},{5,101},{6,30},{7,103},{8,0},{9... | collective-permute-start | bytes 405512 | tf_op jit(solution)/shard_map/ppermute | solution.py:332
  8.1 0.7 copy-start
  12.5 10.9 %collective-permute-start.3 = (bf16[4,528,128]{2,1,0:T(8,128)(2,1)S(1)}, bf16[4,528,128]{2,1,0:T(8,128)(2,1)S(1)}, u32[]{:S(2)}, u32[]{:S(2)}) collective-permute-start(bf16[4,528,128]{2,1,0:T(8,128)(2,1)S(1)} %pad_maximum_fusion.q_ref), channel_id=1, source_target_pairs={{0,32},{1,9},{2,34},{3,11},{4,36},{5,13},{6,38},{7,15},{8,40},{9,1... | collective-permute-start | bytes 1622024 | tf_op jit(solution)/shard_map/ppermute | solution.py:332
  14.2 18.6 %collective-permute-start.5 = (bf16[4,528,128]{2,1,0:T(8,128)(2,1)S(1)}, bf16[4,528,128]{2,1,0:T(8,128)(2,1)S(1)}, u32[]{:S(2)}, u32[]{:S(2)}) collective-permute-start(bf16[4,528,128]{2,1,0:T(8,128)(2,1)S(1)} %pad_maximum_fusion.q_ref), channel_id=1, source_target_pairs={{0,96},{1,25},{2,98},{3,27},{4,100},{5,29},{6,102},{7,31},{8,104},... | collective-permute-start | bytes 1622024 | tf_op jit(solution)/shard_map/ppermute | solution.py:332
  22.1 18.0 %collective-permute-start.7 = (bf16[4,528,128]{2,1,0:T(8,128)(2,1)S(1)}, bf16[4,528,128]{2,1,0:T(8,128)(2,1)S(1)}, u32[]{:S(2)}, u32[]{:S(2)}) collective-permute-start(bf16[4,528,128]{2,1,0:T(8,128)(2,1)S(1)} %pad_maximum_fusion.q_ref), channel_id=1, source_target_pairs={{0,64},{1,17},{2,66},{3,19},{4,68},{5,21},{6,70},{7,23},{8,72},{9,... | collective-permute-start | bytes 1622024 | tf_op jit(solution)/shard_map/ppermute | solution.py:332
  30.6 16.8 %collective-permute-start.4 = (bf16[4,528,128]{2,1,0:T(8,128)(2,1)S(1)}, bf16[4,528,128]{2,1,0:T(8,128)(2,1)S(1)}, u32[]{:S(2)}, u32[]{:S(2)}) collective-permute-start(bf16[4,528,128]{2,1,0:T(8,128)(2,1)S(1)} %attend.5), channel_id=1, source_target_pairs={{0,96},{1,25},{2,98},{3,27},{4,100},{5,29},{6,102},{7,31},{8,104},... | collective-permute-start | bytes 1622024 | tf_op jit(solution)/shard_map/ppermute | solution.py:332
  40.0 9.8 %collective-permute-start.6 = (bf16[4,528,128]{2,1,0:T(8,128)(2,1)S(1)}, bf16[4,528,128]{2,1,0:T(8,128)(2,1)S(1)}, u32[]{:S(2)}, u32[]{:S(2)}) collective-permute-start(bf16[4,528,128]{2,1,0:T(8,128)(2,1)S(1)} %attend.6), channel_id=1, source_target_pairs={{0,32},{1,9},{2,34},{3,11},{4,36},{5,13},{6,38},{7,15},{8,40},{9,1... | collective-permute-start | bytes 1622024 | tf_op jit(solution)/shard_map/ppermute | solution.py:332
  45.8 10.1 %collective-permute-start.8 = (bf16[4,528,128]{2,1,0:T(8,128)(2,1)S(1)}, bf16[4,528,128]{2,1,0:T(8,128)(2,1)S(1)}, u32[]{:S(2)}, u32[]{:S(2)}) collective-permute-start(bf16[4,528,128]{2,1,0:T(8,128)(2,1)S(1)} %attend.7), channel_id=1, source_target_pairs={{0,64},{1,17},{2,66},{3,19},{4,68},{5,21},{6,70},{7,23},{8,72},{9,... | collective-permute-start | bytes 1622024 | tf_op jit(solution)/shard_map/ppermute | solution.py:332
  56.9 6.8 %collective-permute-start.9 = (bf16[528,128]{1,0:T(8,128)(2,1)S(1)}, bf16[528,128]{1,0:T(8,128)(2,1)S(1)}, u32[]{:S(2)}, u32[]{:S(2)}) collective-permute-start(bf16[528,128]{1,0:T(8,128)(2,1)S(1)} %get-tuple-element.29), channel_id=1, source_target_pairs={{0,24},{1,97},{2,26},{3,99},{4,28},{5,101},{6,30},{7,103},{8,0},{9... | collective-permute-start | bytes 405512 | tf_op jit(solution)/shard_map/ppermute | solution.py:332
  60.3 5.5 %collective-permute-start.10 = (bf16[528,128]{1,0:T(8,128)(2,1)S(1)}, bf16[528,128]{1,0:T(8,128)(2,1)S(1)}, u32[]{:S(2)}, u32[]{:S(2)}) collective-permute-start(bf16[528,128]{1,0:T(8,128)(2,1)S(1)} %get-tuple-element.30), channel_id=1, source_target_pairs={{0,16},{1,65},{2,18},{3,67},{4,20},{5,69},{6,22},{7,71},{8,24},{9,... | collective-permute-start | bytes 405512 | tf_op jit(solution)/shard_map/ppermute | solution.py:332
  61.1 5.9 %collective-permute-start.11 = (bf16[528,128]{1,0:T(8,128)(2,1)S(1)}, bf16[528,128]{1,0:T(8,128)(2,1)S(1)}, u32[]{:S(2)}, u32[]{:S(2)}) collective-permute-start(bf16[528,128]{1,0:T(8,128)(2,1)S(1)} %get-tuple-element.31), channel_id=1, source_target_pairs={{0,8},{1,33},{2,10},{3,35},{4,12},{5,37},{6,14},{7,39},{8,16},{9,4... | collective-permute-start | bytes 405512 | tf_op jit(solution)/shard_map/ppermute | solution.py:332
  74.1 10.3 %collective-permute-start.12 = (bf16[32,8192]{1,0:T(8,128)(2,1)S(1)}, bf16[32,8192]{1,0:T(8,128)(2,1)S(1)}, u32[]{:S(2)}, u32[]{:S(2)}) collective-permute-start(bf16[32,8192]{1,0:T(8,128)(2,1)S(1)} %get-tuple-element.34), channel_id=1, source_target_pairs={{0,1},{1,0},{2,3},{3,2},{4,5},{5,4},{6,7},{7,6},{8,9},{9,8},{10,11... | collective-permute-start | bytes 1572872 | tf_op jit(solution)/shard_map/ppermute | solution.py:365
  84.6 6.0 %collective-permute-start.13 = (bf16[8,8192]{1,0:T(8,128)(2,1)S(1)}, bf16[8,8192]{1,0:T(8,128)(2,1)S(1)}, u32[]{:S(2)}, u32[]{:S(2)}) collective-permute-start(bf16[8,8192]{1,0:T(8,128)(2,1)S(1)} %get-tuple-element.35), channel_id=1, source_target_pairs={{0,2},{1,3},{2,4},{3,5},{4,6},{5,7},{6,0},{7,1},{8,10},{9,11},{10,... | collective-permute-start | bytes 393224 | tf_op jit(solution)/shard_map/ppermute | solution.py:373
  85.9 8.5 %collective-permute-start.15 = (bf16[8,8192]{1,0:T(8,128)(2,1)S(1)}, bf16[8,8192]{1,0:T(8,128)(2,1)S(1)}, u32[]{:S(2)}, u32[]{:S(2)}) collective-permute-start(bf16[8,8192]{1,0:T(8,128)(2,1)S(1)} %get-tuple-element.36), channel_id=1, source_target_pairs={{0,4},{1,5},{2,6},{3,7},{4,0},{5,1},{6,2},{7,3},{8,12},{9,13},{10,... | collective-permute-start | bytes 393224 | tf_op jit(solution)/shard_map/ppermute | solution.py:373
  88.3 6.1 %collective-permute-start.14 = (bf16[8,8192]{1,0:T(8,128)(2,1)S(1)}, bf16[8,8192]{1,0:T(8,128)(2,1)S(1)}, u32[]{:S(2)}, u32[]{:S(2)}) collective-permute-start(bf16[8,8192]{1,0:T(8,128)(2,1)S(1)} %get-tuple-element.37), channel_id=1, source_target_pairs={{0,6},{1,7},{2,0},{3,1},{4,2},{5,3},{6,4},{7,5},{8,14},{9,15},{10,... | collective-permute-start | bytes 393224 | tf_op jit(solution)/shard_map/ppermute | solution.py:373

commit v2 on v1

--- a/solution.py
+++ b/solution.py
@@ -41,6 +41,38 @@
 
 def levels(meta, b):
     return meta[3 * b : 3 * b + 1] + meta[3 * b + 1 : 3 * b + 2] + meta[3 * b + 2 : 3 * b + 3]
+
+
+def pack_kernel(q_any, a_any, o_ref, a_ref, meta_ref, q_sem, a_sem):
+    rows = q_any.shape[0]
+    q_copy = pltpu.make_async_copy(q_any, o_ref.at[pl.ds(0, rows)], q_sem)
+    a_copy = pltpu.make_async_copy(a_any, a_ref, a_sem)
+    q_copy.start()
+    a_copy.start()
+    meta_ref[...] = jnp.full(meta_ref.shape, -1.0, F32)
+    a_copy.wait()
+    meta_ref[: a_ref.shape[0], : a_ref.shape[1]] = a_ref[...].astype(F32)
+    o_ref[rows:, :] = meta_ref[...].astype(BF16)
+    q_copy.wait()
+
+
+def pack(q, ancestors):
+    rows, width = q.shape
+    return pl.pallas_call(
+        pack_kernel,
+        out_shape=jax.ShapeDtypeStruct((rows + META, width), BF16),
+        in_specs=[ANY] * 2,
+        out_specs=VMEM,
+        scratch_shapes=[
+            pltpu.VMEM(ancestors.shape, jnp.int32),
+            pltpu.VMEM((META, width), F32),
+            pltpu.SemaphoreType.DMA,
+            pltpu.SemaphoreType.DMA,
+        ],
+        compiler_params=pltpu.CompilerParams(vmem_limit_bytes=4 << 20),
+        cost_estimate=pl.CostEstimate(flops=1 << 10, bytes_accessed=1 << 18, transcendentals=0),
+        name="pack",
+    )(*(pltpu.with_memory_space_constraint(a, pltpu.HBM) for a in (q, ancestors)))
 
 
 def prepare_kernel(scale, group, lengths, *refs):
@@ -102,9 +134,11 @@
 
 
 def attend_kernel(
-    scale, halves, lengths, q_ref, k_ref, v_ref, o_ref, s_ref, m_ref, acc_ref, flag_ref, member, f_sem
+    scale, halves, lengths, q_ref, k_ref, v_ref, *refs
 ):
     homes, held, width = q_ref.shape
+    pieces, (s_ref, m_ref, acc_ref, flag_ref, member, f_sem) = refs[:-6], refs[-6:]
+    o_refs = [piece.at[i] for piece in pieces for i in range(piece.shape[0])]
     rows = held - META
     tiles, _, size = k_ref.shape
     part = rows // halves
@@ -171,22 +205,22 @@
     for h in range(homes):
         here = slice(h * rows, (h + 1) * rows)
         total = acc_ref[here, width:]
-        o_ref[h, :rows, :] = (acc_ref[here, :width] / jnp.maximum(total, -1.0 / NEG)).astype(BF16)
+        o_refs[h][:rows, :] = (acc_ref[here, :width] / jnp.maximum(total, -1.0 / NEG)).astype(BF16)
         sums = jnp.concatenate(to_lanes(total, rows), axis=0)
         peaks = jnp.concatenate(to_lanes(m_ref[here, :], rows), axis=0)
         level = jnp.where(sums > 0.0, peaks + jnp.log(jnp.maximum(sums, -1.0 / NEG)) * LOG2, NEG)
-        o_ref[h, rows:, :] = in_parts([level[b : b + 1] for b in range(rows // 128)])
-
-
-def attend(q, keys, values, lengths, scale, halves):
+        o_refs[h][rows:, :] = in_parts([level[b : b + 1] for b in range(rows // 128)])
+
+
+def attend(q, keys, values, lengths, scale, halves, pieces=1):
     homes, held, width = q.shape
     tiles, _, size = keys.shape
     rows = held - META
     return pl.pallas_call(
         functools.partial(attend_kernel, scale, halves),
-        out_shape=jax.ShapeDtypeStruct(q.shape, BF16),
+        out_shape=[jax.ShapeDtypeStruct((homes // pieces, held, width), BF16)] * pieces,
         in_specs=[SMEM, VMEM, VMEM, VMEM],
-        out_specs=VMEM,
+        out_specs=[VMEM] * pieces,
         scratch_shapes=[
             pltpu.VMEM((tiles, homes * rows, size), F32),
             pltpu.VMEM((homes * rows, 128), F32),
@@ -196,7 +230,7 @@
             pltpu.SemaphoreType.DMA,
         ],
         compiler_params=pltpu.CompilerParams(vmem_limit_bytes=44 << 20),
-        cost_estimate=pl.CostEstimate(flops=1 << 30, bytes_accessed=1 << 20, transcendentals=1 << 18),
+        cost_estimate=pl.CostEstimate(flops=1 << 20, bytes_accessed=1 << 18, transcendentals=0),
         name="attend",
     )(lengths, q, keys, values)
 
@@ -209,37 +243,34 @@
     return (weight / total).T, top + jnp.log(total) * LOG2
 
 
-def merge_kernel(*refs):
-    a_refs, o_refs = refs[:2], refs[2:]
-    count = len(a_refs)
-    homes, held, _ = a_refs[0].shape
+def merge_kernel(first, one_ref, two_ref, *o_refs):
+    homes, held, _ = two_ref.shape
     if len(o_refs) == 1:
         o_refs = [o_refs[0].at[h] for h in range(homes)]
     rows = held - META
     for h in range(homes):
-        metas = [a[h, rows:, :].astype(F32) for a in a_refs]
+        given = [one_ref.at[first + h], two_ref.at[h]]
+        metas = [a[rows:, :].astype(F32) for a in given]
         lines = []
         for b in range(rows // 128):
             weight, line = weights_of([levels(meta, b) for meta in metas])
             lines.append(line)
             here = slice(b * 128, (b + 1) * 128)
-            acc = a_refs[0][h, here, :].astype(F32) * weight[:, 0:1]
-            for i in range(1, count):
-                acc = acc + a_refs[i][h, here, :].astype(F32) * weight[:, i : i + 1]
+            acc = given[0][here, :].astype(F32) * weight[:, 0:1] + given[1][here, :].astype(F32) * weight[:, 1:2]
             o_refs[h][here, :] = acc.astype(BF16)
         o_refs[h][rows:, :] = in_parts(lines)
 
 
-def merge(one, two, apart):
-    homes, held, width = one.shape
-    out = [jax.ShapeDtypeStruct((held, width), BF16)] * homes if apart else jax.ShapeDtypeStruct(one.shape, BF16)
+def merge(one, two, first=0, apart=False):
+    homes, held, width = two.shape
+    out = [jax.ShapeDtypeStruct((held, width), BF16)] * homes if apart else jax.ShapeDtypeStruct(two.shape, BF16)
     return pl.pallas_call(
-        merge_kernel,
+        functools.partial(merge_kernel, first),
         out_shape=out,
         in_specs=[VMEM] * 2,
         out_specs=[VMEM] * homes if apart else VMEM,
         compiler_params=pltpu.CompilerParams(vmem_limit_bytes=16 << 20),
-        cost_estimate=pl.CostEstimate(flops=1 << 34, bytes_accessed=4 << 20, transcendentals=1 << 14),
+        cost_estimate=pl.CostEstimate(flops=1 << 30, bytes_accessed=1 << 18, transcendentals=0),
         name="merge",
     )(one, two)
 
@@ -331,8 +362,7 @@
                 pairs.append((o * ranks + k, to * ranks + k))
         return lax.ppermute(x, ("owner", "kvh"), pairs)
 
-    names = jnp.pad(ancestors.astype(BF16), ((0, META - parts), (0, width - ancestors.shape[1])), constant_values=-1)
-    home = jnp.concatenate([queries.reshape(rows, width), names], axis=0)
+    home = pack(queries.reshape(rows, width), ancestors)
     near = [along(home, 0, d) for d in range(1, side)]
     keys, values, own = prepare(
         tile_lengths,
@@ -344,23 +374,26 @@
         scale,
         group,
     )
-    row, keys, values = lax.optimization_barrier((jnp.stack([home] + near), keys, values))
+    row, keys, values = lax.optimization_barrier((jnp.stack(near + [home]), keys, values))
     order = sorted(range(side), key=lambda e: min(e, side - e))
     blocks = {e: along(row, 1, e) if e else row for e in order[:-1]}
-    back = []
-    for e in order:
-        if e == order[1]:
-            late, out = lax.optimization_barrier((row, out))
+    outs = None
+    for i, e in enumerate(order):
+        if i == 1:
+            late, outs = lax.optimization_barrier((row, outs))
             blocks[order[-1]] = along(late, 1, order[-1])
         block = blocks[e]
         if e:
-            block, out = lax.optimization_barrier((block, out))
-        out = attend(block, keys, values, tile_lengths, scale, parts)
-        back.append(along(out, 1, -e) if e else out)
-    merged = back[0]
-    for i in range(1, side):
-        merged = merge(merged, back[i], i == side - 1)
-    final = [along(merged[d], 0, -d) if d else merged[d] for d in range(side)]
+            block, outs = lax.optimization_barrier((block, outs))
+        last = i == side - 1
+        outs = attend(block, keys, values, tile_lengths, scale, parts, 2 if last else 1)
+        back = [along(out, 1, -e) for out in outs] if e else outs
+        if not last:
+            merged = merge(merged, back[0]) if e else back[0]
+    ready = []
+    for piece in back:
+        ready += merge(merged, piece, len(ready), True)
+    final = [ready[-1]] + [along(ready[d - 1], 0, -d) for d in range(1, side)]
     keep, give = project(final, own, out_weight, group, ranks, cores)
     got = lax.ppermute(give, "kvh", [(k, k // cores * cores + (k + 1) % cores) for k in range(ranks)])
     share = keep.shape[0] // chips

time: 94.4 us -> 85.9 us (0.910); the launches traced: 95.1 us -> 85.2 us
  Pallas kernels: 39.3 us -> 30.2 us
  starting transfers between devices: 33.3 us -> 38.5 us
  waiting for transfers between devices: 19.2 us -> 14.8 us
  other arithmetic: 2.53 us -> 0.9 us
    pallas_call x4, Pallas kernels: 25.7 us -> 15.5 us  [attend(): pl.pallas_call(functools.partial(attend_kernel, scale, halves), out_shape...]
    ppermute x12 -> x13, starting transfers between devices: 19.6 us -> 27 us  [along(): return lax.ppermute(x, ('owner', 'kvh'), pairs)]
    ppermute x12 -> x13, waiting for transfers between devices: 12.7 us -> 8.38 us  [along(): return lax.ppermute(x, ('owner', 'kvh'), pairs)]
    ppermute x1, starting transfers between devices: 8.79 us -> 6.68 us  [local(): lax.ppermute(give, 'kvh', [(k, k // cores * cores + (k + 1) % cores) for...]
    pallas_call x3 -> x5, Pallas kernels: 3.02 us -> 4.1 us  [the longest x4 3.17 us: merge(): pl.pallas_call(functools.partial(merge_kernel, first), out_shape=out, in_...]
  transfers between devices with their start and end apart: 16 -> 17, of which waited for: 9 -> 8; matrix products, arithmetic and copies ran while one was open for 0% -> 0% of each run, Pallas kernels for 33% -> 26%
where the time goes in v2:
time: 85.9 us; the launch traced here: 85.2 us
  starting transfers between devices  38.5 us (45%)
  Pallas kernels  30.2 us (35%)
  waiting for transfers between devices  14.8 us (17%)
  other arithmetic  0.9 us (1%)
    ppermute x13, starting transfers between devices, along(): return lax.ppermute(x, ('owner', 'kvh'), pairs)  27 us
    pallas_call x4, Pallas kernels, attend(): pl.pallas_call(functools.partial(attend_kernel, scale, halves), out_shape...  15.5 us
    ppermute x13, waiting for transfers between devices, along(): return lax.ppermute(x, ('owner', 'kvh'), pairs)  8.38 us
    pallas_call x1, Pallas kernels, project(): pl.pallas_call(functools.partial(project_kernel, group, ranks, cores), ou...  7.04 us
    ppermute x1, starting transfers between devices, local(): lax.ppermute(give, 'kvh', [(k, k // cores * cores + (k + 1) % cores) for...  6.68 us
    ppermute x3, waiting for transfers between devices, local(): lax.ppermute(pieces[d].astype(BF16), 'kvh', pairs).astype(F32)  4.92 us
    ppermute x3, starting transfers between devices, local(): lax.ppermute(pieces[d].astype(BF16), 'kvh', pairs).astype(F32)  4.86 us
    pallas_call x1, Pallas kernels, prepare(): pl.pallas_call(functools.partial(prepare_kernel, scale, group), out_shape...  3.6 us
  transfers between devices with their start and end apart: 17, of which 8 were waited for; matrix products, arithmetic and copies ran while one was open for 0% of the time, Pallas kernels for 26%

profile of v2, /device:TPU:1, one launch (start us, length us, event | category | flops | bytes accessed | tf_op | source)
XLA Modules:
  0.0 85.2 jit_solution(15769133143276671163)
XLA Ops:
  0.9 3.6 %collective-permute-start.2 = (bf16[528,128]{1,0:T(8,128)(2,1)S(1)}, bf16[528,128]{1,0:T(8,128)(2,1)S(1)}, u32[]{:S(2)}, u32[]{:S(2)}) collective-permute-start(bf16[528,128]{1,0:T(8,128)(2,1)S(1)} %pack.1), channel_id=1, source_target_pairs={{0,24},{1,97},{2,26},{3,99},{4,28},{5,101},{6,30},{7,103},{8,0},{9... | collective-permute-start | bytes 405512 | tf_op jit(solution)/shard_map/ppermute | solution.py:363
  6.3 3.6 %prepare.1 = (bf16[6,128,512]{2,1,0:T(8,128)(2,1)S(1)}, bf16[6,512,256]{2,1,0:T(8,128)(2,1)S(1)}, f32[520,128]{1,0:T(8,128)S(1)}) custom-call(s32[6]{0:T(128)S(1)} %copy-done, bf16[2,256,128]{2,1,0:T(8,128)(2,1)} %bitcast.14, bf16[2,32,128]{2,1,0:T(8,128)(2,1)} %bitcast.18, bf16[2,32,128]{2,1,0:T(8,128)(2,1)} %bitcast.19, bf16[6,512,128]{2,1,0:T(8,128)(2,1)} %bitcast.11, ...), custom_call_target="tpu_custom_call" | custom-call | flops 16777216 | bytes 16777216 | tf_op jit(solution)/shard_map/prepare/pallas_call | solution.py:119
  10.0 1.6 %collective-permute-done = bf16[528,128]{1,0:T(8,128)(2,1)S(1)} collective-permute-done((bf16[528,128]{1,0:T(8,128)(2,1)S(1)}, bf16[528,128]{1,0:T(8,128)(2,1)S(1)}, u32[]{:S(2)}, u32[]{:S(2)}) %collective-permute-start) | collective-permute-done | bytes 135200 | tf_op jit(solution)/shard_map/ppermute | solution.py:363
  11.7 1.4 %collective-permute-start.3 = (bf16[4,528,128]{2,1,0:T(8,128)(2,1)S(1)}, bf16[4,528,128]{2,1,0:T(8,128)(2,1)S(1)}, u32[]{:S(2)}, u32[]{:S(2)}) collective-permute-start(bf16[4,528,128]{2,1,0:T(8,128)(2,1)S(1)} %pad_maximum_fusion.q_ref), channel_id=1, source_target_pairs={{0,32},{1,9},{2,34},{3,11},{4,36},{5,13},{6,38},{7,15},{8,40},{9,1... | collective-permute-start | bytes 1622024 | tf_op jit(solution)/shard_map/ppermute | solution.py:363
  13.2 2.2 %collective-permute-start.5 = (bf16[4,528,128]{2,1,0:T(8,128)(2,1)S(1)}, bf16[4,528,128]{2,1,0:T(8,128)(2,1)S(1)}, u32[]{:S(2)}, u32[]{:S(2)}) collective-permute-start(bf16[4,528,128]{2,1,0:T(8,128)(2,1)S(1)} %pad_maximum_fusion.q_ref), channel_id=1, source_target_pairs={{0,96},{1,25},{2,98},{3,27},{4,100},{5,29},{6,102},{7,31},{8,104},... | collective-permute-start | bytes 1622024 | tf_op jit(solution)/shard_map/ppermute | solution.py:363
  15.4 3.9 %attend.4.one_ref = bf16[4,528,128]{2,1,0:T(8,128)(2,1)S(1)} custom-call(s32[6]{0:T(128)S(1)} %copy-done, bf16[4,528,128]{2,1,0:T(8,128)(2,1)S(1)} %pad_maximum_fusion.q_ref, bf16[6,128,512]{2,1,0:T(8,128)(2,1)S(1)} %get-tuple-element.25.k_ref, bf16[6,512,256]{2,1,0:T(8,128)(2,1)S(1)} %get-tuple-element.26.v_ref), custom_call_target="tpu_custom_call" | custom-call | flops 1048576 | bytes 262144 | tf_op jit(solution)/shard_map/attend/pallas_call | solution.py:219
  19.2 4.3 %collective-permute-start.7 = (bf16[4,528,128]{2,1,0:T(8,128)(2,1)S(1)}, bf16[4,528,128]{2,1,0:T(8,128)(2,1)S(1)}, u32[]{:S(2)}, u32[]{:S(2)}) collective-permute-start(bf16[4,528,128]{2,1,0:T(8,128)(2,1)S(1)} %pad_maximum_fusion.q_ref), channel_id=1, source_target_pairs={{0,64},{1,17},{2,66},{3,19},{4,68},{5,21},{6,70},{7,23},{8,72},{9,... | collective-permute-start | bytes 1622024 | tf_op jit(solution)/shard_map/ppermute | solution.py:363
  23.5 3.9 %attend.5 = bf16[4,528,128]{2,1,0:T(8,128)(2,1)S(1)} custom-call(s32[6]{0:T(128)S(1)} %copy-done, bf16[4,528,128]{2,1,0:T(8,128)(2,1)S(1)} %collective-permute-done.3.q_ref, bf16[6,128,512]{2,1,0:T(8,128)(2,1)S(1)} %get-tuple-element.25.k_ref, bf16[6,512,256]{2,1,0:T(8,128)(2,1)S(1)} %get-tuple-element.26.v_ref), custom_call_target="tpu_custom_call" | custom-call | flops 1048576 | bytes 262144 | tf_op jit(solution)/shard_map/attend/pallas_call | solution.py:219
  27.4 2.3 %collective-permute-start.4 = (bf16[4,528,128]{2,1,0:T(8,128)(2,1)S(1)}, bf16[4,528,128]{2,1,0:T(8,128)(2,1)S(1)}, u32[]{:S(2)}, u32[]{:S(2)}) collective-permute-start(bf16[4,528,128]{2,1,0:T(8,128)(2,1)S(1)} %attend.5), channel_id=1, source_target_pairs={{0,96},{1,25},{2,98},{3,27},{4,100},{5,29},{6,102},{7,31},{8,104},... | collective-permute-start | bytes 1622024 | tf_op jit(solution)/shard_map/ppermute | solution.py:363
  29.7 3.9 %attend.6 = bf16[4,528,128]{2,1,0:T(8,128)(2,1)S(1)} custom-call(s32[6]{0:T(128)S(1)} %copy-done, bf16[4,528,128]{2,1,0:T(8,128)(2,1)S(1)} %collective-permute-done.5.q_ref, bf16[6,128,512]{2,1,0:T(8,128)(2,1)S(1)} %get-tuple-element.25.k_ref, bf16[6,512,256]{2,1,0:T(8,128)(2,1)S(1)} %get-tuple-element.26.v_ref), custom_call_target="tpu_custom_call" | custom-call | flops 1048576 | bytes 262144 | tf_op jit(solution)/shard_map/attend/pallas_call | solution.py:219
  33.6 2.4 %collective-permute-start.6 = (bf16[4,528,128]{2,1,0:T(8,128)(2,1)S(1)}, bf16[4,528,128]{2,1,0:T(8,128)(2,1)S(1)}, u32[]{:S(2)}, u32[]{:S(2)}) collective-permute-start(bf16[4,528,128]{2,1,0:T(8,128)(2,1)S(1)} %attend.6), channel_id=1, source_target_pairs={{0,32},{1,9},{2,34},{3,11},{4,36},{5,13},{6,38},{7,15},{8,40},{9,1... | collective-permute-start | bytes 1622024 | tf_op jit(solution)/shard_map/ppermute | solution.py:363
  36.0 3.9 %attend.7 = (bf16[2,528,128]{2,1,0:T(8,128)(2,1)S(1)}, bf16[2,528,128]{2,1,0:T(8,128)(2,1)S(1)}) custom-call(s32[6]{0:T(128)S(1)} %copy-done, bf16[4,528,128]{2,1,0:T(8,128)(2,1)S(1)} %collective-permute-done.7.q_ref, bf16[6,128,512]{2,1,0:T(8,128)(2,1)S(1)} %get-tuple-element.25.k_ref, bf16[6,512,256]{2,1,0:T(8,128)(2,1)S(1)} %get-tuple-element.26.v_ref), custom_call_target="tpu_custom_call" | custom-call | flops 1048576 | bytes 262144 | tf_op jit(solution)/shard_map/attend/pallas_call | solution.py:219
  39.9 5.4 %collective-permute-start.9 = (bf16[2,528,128]{2,1,0:T(8,128)(2,1)S(1)}, bf16[2,528,128]{2,1,0:T(8,128)(2,1)S(1)}, u32[]{:S(2)}, u32[]{:S(2)}) collective-permute-start(bf16[2,528,128]{2,1,0:T(8,128)(2,1)S(1)} %get-tuple-element.32), channel_id=1, source_target_pairs={{0,64},{1,17},{2,66},{3,19},{4,68},{5,21},{6,70},{7,23},{8,72},{9,... | collective-permute-start | bytes 811016 | tf_op jit(solution)/shard_map/ppermute | solution.py:363
  47.4 2.0 %collective-permute-done.9.two_ref = bf16[2,528,128]{2,1,0:T(8,128)(2,1)S(1)} collective-permute-done((bf16[2,528,128]{2,1,0:T(8,128)(2,1)S(1)}, bf16[2,528,128]{2,1,0:T(8,128)(2,1)S(1)}, u32[]{:S(2)}, u32[]{:S(2)}) %collective-permute-start.9) | collective-permute-done | bytes 270368 | tf_op jit(solution)/shard_map/ppermute | solution.py:363
  50.0 1.4 %collective-permute-start.10 = (bf16[528,128]{1,0:T(8,128)(2,1)S(1)}, bf16[528,128]{1,0:T(8,128)(2,1)S(1)}, u32[]{:S(2)}, u32[]{:S(2)}) collective-permute-start(bf16[528,128]{1,0:T(8,128)(2,1)S(1)} %get-tuple-element.33), channel_id=1, source_target_pairs={{0,24},{1,97},{2,26},{3,99},{4,28},{5,101},{6,30},{7,103},{8,0},{9... | collective-permute-start | bytes 405512 | tf_op jit(solution)/shard_map/ppermute | solution.py:363
  51.4 2.0 %collective-permute-start.11 = (bf16[528,128]{1,0:T(8,128)(2,1)S(1)}, bf16[528,128]{1,0:T(8,128)(2,1)S(1)}, u32[]{:S(2)}, u32[]{:S(2)}) collective-permute-start(bf16[528,128]{1,0:T(8,128)(2,1)S(1)} %get-tuple-element.34), channel_id=1, source_target_pairs={{0,16},{1,65},{2,18},{3,67},{4,20},{5,69},{6,22},{7,71},{8,24},{9,... | collective-permute-start | bytes 405512 | tf_op jit(solution)/shard_map/ppermute | solution.py:363
  54.8 2.0 %collective-permute-done.11.refs_2_ = bf16[528,128]{1,0:T(8,128)(2,1)S(1)} collective-permute-done((bf16[528,128]{1,0:T(8,128)(2,1)S(1)}, bf16[528,128]{1,0:T(8,128)(2,1)S(1)}, u32[]{:S(2)}, u32[]{:S(2)}) %collective-permute-start.11) | collective-permute-done | bytes 135200 | tf_op jit(solution)/shard_map/ppermute | solution.py:363
  56.8 2.6 %collective-permute-done.12.refs_3_ = bf16[528,128]{1,0:T(8,128)(2,1)S(1)} collective-permute-done((bf16[528,128]{1,0:T(8,128)(2,1)S(1)}, bf16[528,128]{1,0:T(8,128)(2,1)S(1)}, u32[]{:S(2)}, u32[]{:S(2)}) %collective-permute-start.12) | collective-permute-done | bytes 135200 | tf_op jit(solution)/shard_map/ppermute | solution.py:363
  59.3 7.0 %project.1 = (bf16[32,8192]{1,0:T(8,128)(2,1)S(1)}, bf16[32,8192]{1,0:T(8,128)(2,1)S(1)}) custom-call(bf16[528,128]{1,0:T(8,128)(2,1)S(1)} %get-tuple-element.31.refs_0_, bf16[528,128]{1,0:T(8,128)(2,1)S(1)} %collective-permute-done.10.refs_1_, bf16[528,128]{1,0:T(8,128)(2,1)S(1)} %collective-permute-done.11.refs_2_, ...), custom_call_target="tpu_custom_call" | custom-call | flops 1073741824 | bytes 18874368 | tf_op jit(solution)/shard_map/project/pallas_call | solution.py:322
  66.4 6.7 %collective-permute-start.13 = (bf16[32,8192]{1,0:T(8,128)(2,1)S(1)}, bf16[32,8192]{1,0:T(8,128)(2,1)S(1)}, u32[]{:S(2)}, u32[]{:S(2)}) collective-permute-start(bf16[32,8192]{1,0:T(8,128)(2,1)S(1)} %get-tuple-element.38), channel_id=1, source_target_pairs={{0,1},{1,0},{2,3},{3,2},{4,5},{5,4},{6,7},{7,6},{8,9},{9,8},{10,11... | collective-permute-start | bytes 1572872 | tf_op jit(solution)/shard_map/ppermute | solution.py:398
  73.1 1.5 %collective-permute-done.13 = bf16[32,8192]{1,0:T(8,128)(2,1)S(1)} collective-permute-done((bf16[32,8192]{1,0:T(8,128)(2,1)S(1)}, bf16[32,8192]{1,0:T(8,128)(2,1)S(1)}, u32[]{:S(2)}, u32[]{:S(2)}) %collective-permute-start.13) | collective-permute-done | bytes 524320 | tf_op jit(solution)/shard_map/ppermute | solution.py:398
  74.7 1.3 %collective-permute-start.14 = (bf16[8,8192]{1,0:T(8,128)(2,1)S(1)}, bf16[8,8192]{1,0:T(8,128)(2,1)S(1)}, u32[]{:S(2)}, u32[]{:S(2)}) collective-permute-start(bf16[8,8192]{1,0:T(8,128)(2,1)S(1)} %get-tuple-element.39), channel_id=1, source_target_pairs={{0,2},{1,3},{2,4},{3,5},{4,6},{5,7},{6,0},{7,1},{8,10},{9,11},{10,... | collective-permute-start | bytes 393224 | tf_op jit(solution)/shard_map/ppermute | solution.py:406
  76.0 2.4 %collective-permute-start.16 = (bf16[8,8192]{1,0:T(8,128)(2,1)S(1)}, bf16[8,8192]{1,0:T(8,128)(2,1)S(1)}, u32[]{:S(2)}, u32[]{:S(2)}) collective-permute-start(bf16[8,8192]{1,0:T(8,128)(2,1)S(1)} %get-tuple-element.40), channel_id=1, source_target_pairs={{0,4},{1,5},{2,6},{3,7},{4,0},{5,1},{6,2},{7,3},{8,12},{9,13},{10,... | collective-permute-start | bytes 393224 | tf_op jit(solution)/shard_map/ppermute | solution.py:406
  80.7 3.8 %collective-permute-done.16 = bf16[8,8192]{1,0:T(8,128)(2,1)S(1)} collective-permute-done((bf16[8,8192]{1,0:T(8,128)(2,1)S(1)}, bf16[8,8192]{1,0:T(8,128)(2,1)S(1)}, u32[]{:S(2)}, u32[]{:S(2)}) %collective-permute-start.16) | collective-permute-done | bytes 131104 | tf_op jit(solution)/shard_map/ppermute | solution.py:406
  (26 shorter events, 10.0 us)
Async XLA Ops:
  0.9 8.9 %collective-permute-start.2 = (bf16[528,128]{1,0:T(8,128)(2,1)S(1)}, bf16[528,128]{1,0:T(8,128)(2,1)S(1)}, u32[]{:S(2)}, u32[]{:S(2)}) collective-permute-start(bf16[528,128]{1,0:T(8,128)(2,1)S(1)} %pack.1), channel_id=1, source_target_pairs={{0,24},{1,97},{2,26},{3,99},{4,28},{5,101},{6,30},{7,103},{8,0},{9... | collective-permute-start | bytes 405512 | tf_op jit(solution)/shard_map/ppermute | solution.py:363
  4.6 5.5 %collective-permute-start.1 = (bf16[528,128]{1,0:T(8,128)(2,1)S(1)}, bf16[528,128]{1,0:T(8,128)(2,1)S(1)}, u32[]{:S(2)}, u32[]{:S(2)}) collective-permute-start(bf16[528,128]{1,0:T(8,128)(2,1)S(1)} %pack.1), channel_id=1, source_target_pairs={{0,16},{1,65},{2,18},{3,67},{4,20},{5,69},{6,22},{7,71},{8,24},{9,... | collective-permute-start | bytes 405512 | tf_op jit(solution)/shard_map/ppermute | solution.py:363
  4.9 6.8 %collective-permute-start = (bf16[528,128]{1,0:T(8,128)(2,1)S(1)}, bf16[528,128]{1,0:T(8,128)(2,1)S(1)}, u32[]{:S(2)}, u32[]{:S(2)}) collective-permute-start(bf16[528,128]{1,0:T(8,128)(2,1)S(1)} %pack.1), channel_id=1, source_target_pairs={{0,8},{1,33},{2,10},{3,35},{4,12},{5,37},{6,14},{7,39},{8,16},{9,4... | collective-permute-start | bytes 405512 | tf_op jit(solution)/shard_map/ppermute | solution.py:363
  5.6 0.7 copy-start
  11.7 11.8 %collective-permute-start.3 = (bf16[4,528,128]{2,1,0:T(8,128)(2,1)S(1)}, bf16[4,528,128]{2,1,0:T(8,128)(2,1)S(1)}, u32[]{:S(2)}, u32[]{:S(2)}) collective-permute-start(bf16[4,528,128]{2,1,0:T(8,128)(2,1)S(1)} %pad_maximum_fusion.q_ref), channel_id=1, source_target_pairs={{0,32},{1,9},{2,34},{3,11},{4,36},{5,13},{6,38},{7,15},{8,40},{9,1... | collective-permute-start | bytes 1622024 | tf_op jit(solution)/shard_map/ppermute | solution.py:363
  13.2 16.6 %collective-permute-start.5 = (bf16[4,528,128]{2,1,0:T(8,128)(2,1)S(1)}, bf16[4,528,128]{2,1,0:T(8,128)(2,1)S(1)}, u32[]{:S(2)}, u32[]{:S(2)}) collective-permute-start(bf16[4,528,128]{2,1,0:T(8,128)(2,1)S(1)} %pad_maximum_fusion.q_ref), channel_id=1, source_target_pairs={{0,96},{1,25},{2,98},{3,27},{4,100},{5,29},{6,102},{7,31},{8,104},... | collective-permute-start | bytes 1622024 | tf_op jit(solution)/shard_map/ppermute | solution.py:363
  19.2 16.8 %collective-permute-start.7 = (bf16[4,528,128]{2,1,0:T(8,128)(2,1)S(1)}, bf16[4,528,128]{2,1,0:T(8,128)(2,1)S(1)}, u32[]{:S(2)}, u32[]{:S(2)}) collective-permute-start(bf16[4,528,128]{2,1,0:T(8,128)(2,1)S(1)} %pad_maximum_fusion.q_ref), channel_id=1, source_target_pairs={{0,64},{1,17},{2,66},{3,19},{4,68},{5,21},{6,70},{7,23},{8,72},{9,... | collective-permute-start | bytes 1622024 | tf_op jit(solution)/shard_map/ppermute | solution.py:363
  27.4 18.0 %collective-permute-start.4 = (bf16[4,528,128]{2,1,0:T(8,128)(2,1)S(1)}, bf16[4,528,128]{2,1,0:T(8,128)(2,1)S(1)}, u32[]{:S(2)}, u32[]{:S(2)}) collective-permute-start(bf16[4,528,128]{2,1,0:T(8,128)(2,1)S(1)} %attend.5), channel_id=1, source_target_pairs={{0,96},{1,25},{2,98},{3,27},{4,100},{5,29},{6,102},{7,31},{8,104},... | collective-permute-start | bytes 1622024 | tf_op jit(solution)/shard_map/ppermute | solution.py:363
  33.6 12.8 %collective-permute-start.6 = (bf16[4,528,128]{2,1,0:T(8,128)(2,1)S(1)}, bf16[4,528,128]{2,1,0:T(8,128)(2,1)S(1)}, u32[]{:S(2)}, u32[]{:S(2)}) collective-permute-start(bf16[4,528,128]{2,1,0:T(8,128)(2,1)S(1)} %attend.6), channel_id=1, source_target_pairs={{0,32},{1,9},{2,34},{3,11},{4,36},{5,13},{6,38},{7,15},{8,40},{9,1... | collective-permute-start | bytes 1622024 | tf_op jit(solution)/shard_map/ppermute | solution.py:363
  39.9 9.5 %collective-permute-start.9 = (bf16[2,528,128]{2,1,0:T(8,128)(2,1)S(1)}, bf16[2,528,128]{2,1,0:T(8,128)(2,1)S(1)}, u32[]{:S(2)}, u32[]{:S(2)}) collective-permute-start(bf16[2,528,128]{2,1,0:T(8,128)(2,1)S(1)} %get-tuple-element.32), channel_id=1, source_target_pairs={{0,64},{1,17},{2,66},{3,19},{4,68},{5,21},{6,70},{7,23},{8,72},{9,... | collective-permute-start | bytes 811016 | tf_op jit(solution)/shard_map/ppermute | solution.py:363
  45.3 8.1 %collective-permute-start.8 = (bf16[2,528,128]{2,1,0:T(8,128)(2,1)S(1)}, bf16[2,528,128]{2,1,0:T(8,128)(2,1)S(1)}, u32[]{:S(2)}, u32[]{:S(2)}) collective-permute-start(bf16[2,528,128]{2,1,0:T(8,128)(2,1)S(1)} %get-tuple-element.30), channel_id=1, source_target_pairs={{0,64},{1,17},{2,66},{3,19},{4,68},{5,21},{6,70},{7,23},{8,72},{9,... | collective-permute-start | bytes 811016 | tf_op jit(solution)/shard_map/ppermute | solution.py:363
  50.0 4.8 %collective-permute-start.10 = (bf16[528,128]{1,0:T(8,128)(2,1)S(1)}, bf16[528,128]{1,0:T(8,128)(2,1)S(1)}, u32[]{:S(2)}, u32[]{:S(2)}) collective-permute-start(bf16[528,128]{1,0:T(8,128)(2,1)S(1)} %get-tuple-element.33), channel_id=1, source_target_pairs={{0,24},{1,97},{2,26},{3,99},{4,28},{5,101},{6,30},{7,103},{8,0},{9... | collective-permute-start | bytes 405512 | tf_op jit(solution)/shard_map/ppermute | solution.py:363
  51.4 5.4 %collective-permute-start.11 = (bf16[528,128]{1,0:T(8,128)(2,1)S(1)}, bf16[528,128]{1,0:T(8,128)(2,1)S(1)}, u32[]{:S(2)}, u32[]{:S(2)}) collective-permute-start(bf16[528,128]{1,0:T(8,128)(2,1)S(1)} %get-tuple-element.34), channel_id=1, source_target_pairs={{0,16},{1,65},{2,18},{3,67},{4,20},{5,69},{6,22},{7,71},{8,24},{9,... | collective-permute-start | bytes 405512 | tf_op jit(solution)/shard_map/ppermute | solution.py:363
  54.0 5.4 %collective-permute-start.12 = (bf16[528,128]{1,0:T(8,128)(2,1)S(1)}, bf16[528,128]{1,0:T(8,128)(2,1)S(1)}, u32[]{:S(2)}, u32[]{:S(2)}) collective-permute-start(bf16[528,128]{1,0:T(8,128)(2,1)S(1)} %get-tuple-element.35), channel_id=1, source_target_pairs={{0,8},{1,33},{2,10},{3,35},{4,12},{5,37},{6,14},{7,39},{8,16},{9,4... | collective-permute-start | bytes 405512 | tf_op jit(solution)/shard_map/ppermute | solution.py:363
  66.4 8.2 %collective-permute-start.13 = (bf16[32,8192]{1,0:T(8,128)(2,1)S(1)}, bf16[32,8192]{1,0:T(8,128)(2,1)S(1)}, u32[]{:S(2)}, u32[]{:S(2)}) collective-permute-start(bf16[32,8192]{1,0:T(8,128)(2,1)S(1)} %get-tuple-element.38), channel_id=1, source_target_pairs={{0,1},{1,0},{2,3},{3,2},{4,5},{5,4},{6,7},{7,6},{8,9},{9,8},{10,11... | collective-permute-start | bytes 1572872 | tf_op jit(solution)/shard_map/ppermute | solution.py:398
  74.7 6.0 %collective-permute-start.14 = (bf16[8,8192]{1,0:T(8,128)(2,1)S(1)}, bf16[8,8192]{1,0:T(8,128)(2,1)S(1)}, u32[]{:S(2)}, u32[]{:S(2)}) collective-permute-start(bf16[8,8192]{1,0:T(8,128)(2,1)S(1)} %get-tuple-element.39), channel_id=1, source_target_pairs={{0,2},{1,3},{2,4},{3,5},{4,6},{5,7},{6,0},{7,1},{8,10},{9,11},{10,... | collective-permute-start | bytes 393224 | tf_op jit(solution)/shard_map/ppermute | solution.py:406
  76.0 8.5 %collective-permute-start.16 = (bf16[8,8192]{1,0:T(8,128)(2,1)S(1)}, bf16[8,8192]{1,0:T(8,128)(2,1)S(1)}, u32[]{:S(2)}, u32[]{:S(2)}) collective-permute-start(bf16[8,8192]{1,0:T(8,128)(2,1)S(1)} %get-tuple-element.40), channel_id=1, source_target_pairs={{0,4},{1,5},{2,6},{3,7},{4,0},{5,1},{6,2},{7,3},{8,12},{9,13},{10,... | collective-permute-start | bytes 393224 | tf_op jit(solution)/shard_map/ppermute | solution.py:406
  78.4 6.1 %collective-permute-start.15 = (bf16[8,8192]{1,0:T(8,128)(2,1)S(1)}, bf16[8,8192]{1,0:T(8,128)(2,1)S(1)}, u32[]{:S(2)}, u32[]{:S(2)}) collective-permute-start(bf16[8,8192]{1,0:T(8,128)(2,1)S(1)} %get-tuple-element.41), channel_id=1, source_target_pairs={{0,6},{1,7},{2,0},{3,1},{4,2},{5,3},{6,4},{7,5},{8,14},{9,15},{10,... | collective-permute-start | bytes 393224 | tf_op jit(solution)/shard_map/ppermute | solution.py:406

commit v3 on v2

--- a/solution.py
+++ b/solution.py
@@ -11,6 +11,7 @@
 NEG = -1e30
 META = 16
 STEP = 256
+FEW = 2
 F32 = jnp.float32
 BF16 = jnp.bfloat16
 VMEM = pl.BlockSpec(memory_space=pltpu.VMEM)
@@ -137,7 +138,7 @@
     scale, halves, lengths, q_ref, k_ref, v_ref, *refs
 ):
     homes, held, width = q_ref.shape
-    pieces, (s_ref, m_ref, acc_ref, flag_ref, member, f_sem) = refs[:-6], refs[-6:]
+    pieces, (s_ref, m_ref, acc_ref, member) = refs[:-4], refs[-4:]
     o_refs = [piece.at[i] for piece in pieces for i in range(piece.shape[0])]
     rows = held - META
     tiles, _, size = k_ref.shape
@@ -145,61 +146,71 @@
     count = homes * halves
 
     names = jnp.concatenate([q_ref[h, rows:, :].astype(F32)[:halves] for h in range(homes)], axis=0)
-    lane = lax.broadcasted_iota(jnp.int32, names.shape, 1)
     first = (lax.axis_index("owner") * tiles).astype(F32)
-    flags = jnp.zeros(names.shape, F32)
+    bit = lax.broadcasted_iota(jnp.int32, (count, 1), 0)
     for t in range(tiles):
         inside = jnp.max(jnp.where(names == first + t, 1.0, 0.0), axis=1, keepdims=True)
-        flags = jnp.where(lane == t, inside, flags)
-    flag_ref[:count, :] = flags.astype(jnp.int32)
-    flag_ref[count:, :] = jnp.broadcast_to(jnp.sum(flags, axis=0, keepdims=True), names.shape).astype(jnp.int32)
-    f_copy = pltpu.make_async_copy(flag_ref, member, f_sem)
-    f_copy.start()
+        power = (1 << bit).astype(F32)
+        member[t] = jnp.sum(inside * power).astype(jnp.int32)
+        member[tiles + t] = jnp.sum(inside).astype(jnp.int32)
     m_ref[...] = jnp.full(m_ref.shape, NEG, F32)
     acc_ref[...] = jnp.zeros(acc_ref.shape, F32)
-    f_copy.wait()
-
-    def blocks(t):
-        return [(slice(i * part, (i + 1) * part), member[i, t] > 0) for i in range(count)]
 
     def for_each_tile(body):
         @pl.loop(0, tiles)
         def _(t):
-            used = member[count, t] > 0
+            held_by = member[t]
+            number = member[tiles + t]
             for n in range(1, size // STEP + 1):
                 fits = lengths[t] > (n - 1) * STEP
                 if n * STEP < size:
                     fits = fits & (lengths[t] <= n * STEP)
 
-                @pl.when(used & fits)
+                @pl.when(fits & (number > FEW))
                 def _():
-                    body(t, n * STEP)
-
-    def score(t, wide):
-        q = q_ref[:, :rows, :].reshape(homes * rows, width)
+                    every = [(slice(i * part, (i + 1) * part), (held_by >> i) & 1 > 0) for i in range(count)]
+                    body(t, n * STEP, q_ref[:, :rows, :].reshape(homes * rows, width), slice(None), every)
+
+                @pl.when(fits & (number > 0) & (number <= FEW))
+                def _():
+                    @pl.loop(0, count)
+                    def _(i):
+                        @pl.when((held_by >> i) & 1 > 0)
+                        def _():
+                            q = q_ref[i // halves, pl.ds(pl.multiple_of(i % halves * part, part), part), :]
+                            body(t, n * STEP, q, pl.ds(pl.multiple_of(i * part, part), part), [(slice(None), True)])
+
+    def score(t, wide, q, span, blocks):
         s = jnp.dot(q, k_ref[t, :, :wide], preferred_element_type=F32)
-        s_ref[t, :, :wide] = s
-        for here, inside in blocks(t):
+        s_ref[t, span, :wide] = s
+        for here, inside in blocks:
             x = s[here, :128]
             for j in range(128, wide, 128):
                 x = jnp.maximum(x, s[here, j : j + 128])
-            m_ref[here, :] = jnp.maximum(m_ref[here, :], jnp.where(inside, x, NEG))
+            if inside is True:
+                m_ref[span, :] = jnp.maximum(m_ref[span, :], x)
+            else:
+                m_ref[here, :] = jnp.maximum(m_ref[here, :], jnp.where(inside, x, NEG))
 
     for_each_tile(score)
     peak = jnp.max(m_ref[...], axis=1, keepdims=True) * scale
     m_ref[...] = jnp.broadcast_to(peak, m_ref.shape)
 
-    def weigh(t, wide):
+    def weigh(t, wide, q, span, blocks):
         weights = []
-        for here, inside in blocks(t):
-            shift = jnp.where(inside, m_ref[here, :], -NEG)
+        for here, inside in blocks:
+            rows_here = span if inside is True else here
+            shift = m_ref[rows_here, :]
+            if inside is not True:
+                shift = jnp.where(inside, shift, -NEG)
             weights.append(
                 jnp.concatenate(
-                    [jnp.exp2(s_ref[t, here, j : j + 128] * scale - shift).astype(BF16) for j in range(0, wide, 128)],
+                    [jnp.exp2(s_ref[t, rows_here, j : j + 128] * scale - shift).astype(BF16) for j in range(0, wide, 128)],
                     axis=1,
                 )
             )
-        acc_ref[...] += jnp.dot(jnp.concatenate(weights, axis=0), v_ref[t, :wide, :], preferred_element_type=F32)
+        weights = weights[0] if len(weights) == 1 else jnp.concatenate(weights, axis=0)
+        acc_ref[span, :] += jnp.dot(weights, v_ref[t, :wide, :], preferred_element_type=F32)
 
     for_each_tile(weigh)
     for h in range(homes):
@@ -225,9 +236,7 @@
             pltpu.VMEM((tiles, homes * rows, size), F32),
             pltpu.VMEM((homes * rows, 128), F32),
             pltpu.VMEM((homes * rows, 2 * width), F32),
-            pltpu.VMEM((2 * homes * halves, 128), jnp.int32),
-            pltpu.SMEM((2 * homes * halves, 128), jnp.int32),
-            pltpu.SemaphoreType.DMA,
+            pltpu.SMEM((2 * tiles,), jnp.int32),
         ],
         compiler_params=pltpu.CompilerParams(vmem_limit_bytes=44 << 20),
         cost_estimate=pl.CostEstimate(flops=1 << 20, bytes_accessed=1 << 18, transcendentals=0),

time: 85.9 us -> 82.3 us (0.958)
  starting transfers between devices: 38.5 us -> 33.5 us
  waiting for transfers between devices: 14.8 us -> 16.1 us
    ppermute x1, starting transfers between devices: 6.68 us -> 2.96 us  [local(): lax.ppermute(give, 'kvh', [(k, k // cores * cores + (k + 1) % cores) for...]
    ppermute x13, waiting for transfers between devices: 8.38 us -> 9.73 us  [along(): return lax.ppermute(x, ('owner', 'kvh'), pairs)]
    ppermute x13, starting transfers between devices: 27 us -> 25.6 us  [along(): return lax.ppermute(x, ('owner', 'kvh'), pairs)]
  transfers between devices with their start and end apart: 17 -> 17, of which waited for: 8 -> 10; matrix products, arithmetic and copies ran while one was open for 0% -> 0% of each run, Pallas kernels for 26% -> 27%
where the time goes in v3:
time: 82.3 us; the launch traced here: 81.4 us
  starting transfers between devices  33.5 us (41%)
  Pallas kernels  30.1 us (37%)
  waiting for transfers between devices  16.1 us (20%)
  other arithmetic  0.9 us (1%)
    ppermute x13, starting transfers between devices, along(): return lax.ppermute(x, ('owner', 'kvh'), pairs)  25.6 us
    pallas_call x4, Pallas kernels, attend(): pl.pallas_call(functools.partial(attend_kernel, scale, halves), out_shape...  15.4 us
    ppermute x13, waiting for transfers between devices, along(): return lax.ppermute(x, ('owner', 'kvh'), pairs)  9.73 us
    pallas_call x1, Pallas kernels, project(): pl.pallas_call(functools.partial(project_kernel, group, ranks, cores), ou...  7.04 us
    ppermute x3, starting transfers between devices, local(): lax.ppermute(pieces[d].astype(BF16), 'kvh', pairs).astype(F32)  4.89 us
    ppermute x3, waiting for transfers between devices, local(): lax.ppermute(pieces[d].astype(BF16), 'kvh', pairs).astype(F32)  4.86 us
    pallas_call x1, Pallas kernels, prepare(): pl.pallas_call(functools.partial(prepare_kernel, scale, group), out_shape...  3.6 us
    pallas_call x4, Pallas kernels, merge(): pl.pallas_call(functools.partial(merge_kernel, first), out_shape=out, in_...  3.17 us
  transfers between devices with their start and end apart: 17, of which 10 were waited for; matrix products, arithmetic and copies ran while one was open for 0% of the time, Pallas kernels for 27%

profile of v3, /device:TPU:1, one launch (start us, length us, event | category | flops | bytes accessed | tf_op | source)
XLA Modules:
  0.0 81.4 jit_solution(1085001690580402)
XLA Ops:
  0.9 3.6 %collective-permute-start.2 = (bf16[528,128]{1,0:T(8,128)(2,1)S(1)}, bf16[528,128]{1,0:T(8,128)(2,1)S(1)}, u32[]{:S(2)}, u32[]{:S(2)}) collective-permute-start(bf16[528,128]{1,0:T(8,128)(2,1)S(1)} %pack.1), channel_id=1, source_target_pairs={{0,24},{1,97},{2,26},{3,99},{4,28},{5,101},{6,30},{7,103},{8,0},{9... | collective-permute-start | bytes 405512 | tf_op jit(solution)/shard_map/ppermute | solution.py:372
  6.3 3.6 %prepare.1 = (bf16[6,128,512]{2,1,0:T(8,128)(2,1)S(1)}, bf16[6,512,256]{2,1,0:T(8,128)(2,1)S(1)}, f32[520,128]{1,0:T(8,128)S(1)}) custom-call(s32[6]{0:T(128)S(1)} %copy-done, bf16[2,256,128]{2,1,0:T(8,128)(2,1)} %bitcast.14, bf16[2,32,128]{2,1,0:T(8,128)(2,1)} %bitcast.18, bf16[2,32,128]{2,1,0:T(8,128)(2,1)} %bitcast.19, bf16[6,512,128]{2,1,0:T(8,128)(2,1)} %bitcast.11, ...), custom_call_target="tpu_custom_call" | custom-call | flops 16777216 | bytes 16777216 | tf_op jit(solution)/shard_map/prepare/pallas_call | solution.py:120
  10.0 1.6 %collective-permute-done = bf16[528,128]{1,0:T(8,128)(2,1)S(1)} collective-permute-done((bf16[528,128]{1,0:T(8,128)(2,1)S(1)}, bf16[528,128]{1,0:T(8,128)(2,1)S(1)}, u32[]{:S(2)}, u32[]{:S(2)}) %collective-permute-start) | collective-permute-done | bytes 135200 | tf_op jit(solution)/shard_map/ppermute | solution.py:372
  11.7 1.4 %collective-permute-start.3 = (bf16[4,528,128]{2,1,0:T(8,128)(2,1)S(1)}, bf16[4,528,128]{2,1,0:T(8,128)(2,1)S(1)}, u32[]{:S(2)}, u32[]{:S(2)}) collective-permute-start(bf16[4,528,128]{2,1,0:T(8,128)(2,1)S(1)} %pad_maximum_fusion.q_ref), channel_id=1, source_target_pairs={{0,32},{1,9},{2,34},{3,11},{4,36},{5,13},{6,38},{7,15},{8,40},{9,1... | collective-permute-start | bytes 1622024 | tf_op jit(solution)/shard_map/ppermute | solution.py:372
  13.2 2.2 %collective-permute-start.5 = (bf16[4,528,128]{2,1,0:T(8,128)(2,1)S(1)}, bf16[4,528,128]{2,1,0:T(8,128)(2,1)S(1)}, u32[]{:S(2)}, u32[]{:S(2)}) collective-permute-start(bf16[4,528,128]{2,1,0:T(8,128)(2,1)S(1)} %pad_maximum_fusion.q_ref), channel_id=1, source_target_pairs={{0,96},{1,25},{2,98},{3,27},{4,100},{5,29},{6,102},{7,31},{8,104},... | collective-permute-start | bytes 1622024 | tf_op jit(solution)/shard_map/ppermute | solution.py:372
  15.4 4.3 %attend.4.one_ref = bf16[4,528,128]{2,1,0:T(8,128)(2,1)S(1)} custom-call(s32[6]{0:T(128)S(1)} %copy-done, bf16[4,528,128]{2,1,0:T(8,128)(2,1)S(1)} %pad_maximum_fusion.q_ref, bf16[6,128,512]{2,1,0:T(8,128)(2,1)S(1)} %get-tuple-element.25.k_ref, bf16[6,512,256]{2,1,0:T(8,128)(2,1)S(1)} %get-tuple-element.26.v_ref), custom_call_target="tpu_custom_call" | custom-call | flops 1048576 | bytes 262144 | tf_op jit(solution)/shard_map/attend/pallas_call | solution.py:230
  19.7 2.7 %collective-permute-start.7 = (bf16[4,528,128]{2,1,0:T(8,128)(2,1)S(1)}, bf16[4,528,128]{2,1,0:T(8,128)(2,1)S(1)}, u32[]{:S(2)}, u32[]{:S(2)}) collective-permute-start(bf16[4,528,128]{2,1,0:T(8,128)(2,1)S(1)} %pad_maximum_fusion.q_ref), channel_id=1, source_target_pairs={{0,64},{1,17},{2,66},{3,19},{4,68},{5,21},{6,70},{7,23},{8,72},{9,... | collective-permute-start | bytes 1622024 | tf_op jit(solution)/shard_map/ppermute | solution.py:372
  22.3 4.3 %attend.5 = bf16[4,528,128]{2,1,0:T(8,128)(2,1)S(1)} custom-call(s32[6]{0:T(128)S(1)} %copy-done, bf16[4,528,128]{2,1,0:T(8,128)(2,1)S(1)} %collective-permute-done.3.q_ref, bf16[6,128,512]{2,1,0:T(8,128)(2,1)S(1)} %get-tuple-element.25.k_ref, bf16[6,512,256]{2,1,0:T(8,128)(2,1)S(1)} %get-tuple-element.26.v_ref), custom_call_target="tpu_custom_call" | custom-call | flops 1048576 | bytes 262144 | tf_op jit(solution)/shard_map/attend/pallas_call | solution.py:230
  26.6 2.7 %collective-permute-start.4 = (bf16[4,528,128]{2,1,0:T(8,128)(2,1)S(1)}, bf16[4,528,128]{2,1,0:T(8,128)(2,1)S(1)}, u32[]{:S(2)}, u32[]{:S(2)}) collective-permute-start(bf16[4,528,128]{2,1,0:T(8,128)(2,1)S(1)} %attend.5), channel_id=1, source_target_pairs={{0,96},{1,25},{2,98},{3,27},{4,100},{5,29},{6,102},{7,31},{8,104},... | collective-permute-start | bytes 1622024 | tf_op jit(solution)/shard_map/ppermute | solution.py:372
  29.3 3.4 %attend.6 = bf16[4,528,128]{2,1,0:T(8,128)(2,1)S(1)} custom-call(s32[6]{0:T(128)S(1)} %copy-done, bf16[4,528,128]{2,1,0:T(8,128)(2,1)S(1)} %collective-permute-done.5.q_ref, bf16[6,128,512]{2,1,0:T(8,128)(2,1)S(1)} %get-tuple-element.25.k_ref, bf16[6,512,256]{2,1,0:T(8,128)(2,1)S(1)} %get-tuple-element.26.v_ref), custom_call_target="tpu_custom_call" | custom-call | flops 1048576 | bytes 262144 | tf_op jit(solution)/shard_map/attend/pallas_call | solution.py:230
  32.7 1.7 %collective-permute-start.6 = (bf16[4,528,128]{2,1,0:T(8,128)(2,1)S(1)}, bf16[4,528,128]{2,1,0:T(8,128)(2,1)S(1)}, u32[]{:S(2)}, u32[]{:S(2)}) collective-permute-start(bf16[4,528,128]{2,1,0:T(8,128)(2,1)S(1)} %attend.6), channel_id=1, source_target_pairs={{0,32},{1,9},{2,34},{3,11},{4,36},{5,13},{6,38},{7,15},{8,40},{9,1... | collective-permute-start | bytes 1622024 | tf_op jit(solution)/shard_map/ppermute | solution.py:372
  34.4 3.4 %attend.7 = (bf16[2,528,128]{2,1,0:T(8,128)(2,1)S(1)}, bf16[2,528,128]{2,1,0:T(8,128)(2,1)S(1)}) custom-call(s32[6]{0:T(128)S(1)} %copy-done, bf16[4,528,128]{2,1,0:T(8,128)(2,1)S(1)} %collective-permute-done.7.q_ref, bf16[6,128,512]{2,1,0:T(8,128)(2,1)S(1)} %get-tuple-element.25.k_ref, bf16[6,512,256]{2,1,0:T(8,128)(2,1)S(1)} %get-tuple-element.26.v_ref), custom_call_target="tpu_custom_call" | custom-call | flops 1048576 | bytes 262144 | tf_op jit(solution)/shard_map/attend/pallas_call | solution.py:230
  37.8 3.2 %collective-permute-start.9 = (bf16[2,528,128]{2,1,0:T(8,128)(2,1)S(1)}, bf16[2,528,128]{2,1,0:T(8,128)(2,1)S(1)}, u32[]{:S(2)}, u32[]{:S(2)}) collective-permute-start(bf16[2,528,128]{2,1,0:T(8,128)(2,1)S(1)} %get-tuple-element.32), channel_id=1, source_target_pairs={{0,64},{1,17},{2,66},{3,19},{4,68},{5,21},{6,70},{7,23},{8,72},{9,... | collective-permute-start | bytes 811016 | tf_op jit(solution)/shard_map/ppermute | solution.py:372
  43.5 2.2 %collective-permute-done.9.two_ref = bf16[2,528,128]{2,1,0:T(8,128)(2,1)S(1)} collective-permute-done((bf16[2,528,128]{2,1,0:T(8,128)(2,1)S(1)}, bf16[2,528,128]{2,1,0:T(8,128)(2,1)S(1)}, u32[]{:S(2)}, u32[]{:S(2)}) %collective-permute-start.9) | collective-permute-done | bytes 270368 | tf_op jit(solution)/shard_map/ppermute | solution.py:372
  46.2 5.2 %collective-permute-start.10 = (bf16[528,128]{1,0:T(8,128)(2,1)S(1)}, bf16[528,128]{1,0:T(8,128)(2,1)S(1)}, u32[]{:S(2)}, u32[]{:S(2)}) collective-permute-start(bf16[528,128]{1,0:T(8,128)(2,1)S(1)} %get-tuple-element.33), channel_id=1, source_target_pairs={{0,24},{1,97},{2,26},{3,99},{4,28},{5,101},{6,30},{7,103},{8,0},{9... | collective-permute-start | bytes 405512 | tf_op jit(solution)/shard_map/ppermute | solution.py:372
  51.4 1.6 %collective-permute-start.11 = (bf16[528,128]{1,0:T(8,128)(2,1)S(1)}, bf16[528,128]{1,0:T(8,128)(2,1)S(1)}, u32[]{:S(2)}, u32[]{:S(2)}) collective-permute-start(bf16[528,128]{1,0:T(8,128)(2,1)S(1)} %get-tuple-element.34), channel_id=1, source_target_pairs={{0,16},{1,65},{2,18},{3,67},{4,20},{5,69},{6,22},{7,71},{8,24},{9,... | collective-permute-start | bytes 405512 | tf_op jit(solution)/shard_map/ppermute | solution.py:372
  54.7 2.1 %collective-permute-done.11.refs_2_ = bf16[528,128]{1,0:T(8,128)(2,1)S(1)} collective-permute-done((bf16[528,128]{1,0:T(8,128)(2,1)S(1)}, bf16[528,128]{1,0:T(8,128)(2,1)S(1)}, u32[]{:S(2)}, u32[]{:S(2)}) %collective-permute-start.11) | collective-permute-done | bytes 135200 | tf_op jit(solution)/shard_map/ppermute | solution.py:372
  56.8 2.4 %collective-permute-done.12.refs_3_ = bf16[528,128]{1,0:T(8,128)(2,1)S(1)} collective-permute-done((bf16[528,128]{1,0:T(8,128)(2,1)S(1)}, bf16[528,128]{1,0:T(8,128)(2,1)S(1)}, u32[]{:S(2)}, u32[]{:S(2)}) %collective-permute-start.12) | collective-permute-done | bytes 135200 | tf_op jit(solution)/shard_map/ppermute | solution.py:372
  59.2 7.0 %project.1 = (bf16[32,8192]{1,0:T(8,128)(2,1)S(1)}, bf16[32,8192]{1,0:T(8,128)(2,1)S(1)}) custom-call(bf16[528,128]{1,0:T(8,128)(2,1)S(1)} %get-tuple-element.31.refs_0_, bf16[528,128]{1,0:T(8,128)(2,1)S(1)} %collective-permute-done.10.refs_1_, bf16[528,128]{1,0:T(8,128)(2,1)S(1)} %collective-permute-done.11.refs_2_, ...), custom_call_target="tpu_custom_call" | custom-call | flops 1073741824 | bytes 18874368 | tf_op jit(solution)/shard_map/project/pallas_call | solution.py:331
  66.3 3.0 %collective-permute-start.13 = (bf16[32,8192]{1,0:T(8,128)(2,1)S(1)}, bf16[32,8192]{1,0:T(8,128)(2,1)S(1)}, u32[]{:S(2)}, u32[]{:S(2)}) collective-permute-start(bf16[32,8192]{1,0:T(8,128)(2,1)S(1)} %get-tuple-element.38), channel_id=1, source_target_pairs={{0,1},{1,0},{2,3},{3,2},{4,5},{5,4},{6,7},{7,6},{8,9},{9,8},{10,11... | collective-permute-start | bytes 1572872 | tf_op jit(solution)/shard_map/ppermute | solution.py:407
  69.3 1.5 %collective-permute-done.13 = bf16[32,8192]{1,0:T(8,128)(2,1)S(1)} collective-permute-done((bf16[32,8192]{1,0:T(8,128)(2,1)S(1)}, bf16[32,8192]{1,0:T(8,128)(2,1)S(1)}, u32[]{:S(2)}, u32[]{:S(2)}) %collective-permute-start.13) | collective-permute-done | bytes 524320 | tf_op jit(solution)/shard_map/ppermute | solution.py:407
  70.9 1.3 %collective-permute-start.14 = (bf16[8,8192]{1,0:T(8,128)(2,1)S(1)}, bf16[8,8192]{1,0:T(8,128)(2,1)S(1)}, u32[]{:S(2)}, u32[]{:S(2)}) collective-permute-start(bf16[8,8192]{1,0:T(8,128)(2,1)S(1)} %get-tuple-element.39), channel_id=1, source_target_pairs={{0,2},{1,3},{2,4},{3,5},{4,6},{5,7},{6,0},{7,1},{8,10},{9,11},{10,... | collective-permute-start | bytes 393224 | tf_op jit(solution)/shard_map/ppermute | solution.py:415
  72.2 2.4 %collective-permute-start.16 = (bf16[8,8192]{1,0:T(8,128)(2,1)S(1)}, bf16[8,8192]{1,0:T(8,128)(2,1)S(1)}, u32[]{:S(2)}, u32[]{:S(2)}) collective-permute-start(bf16[8,8192]{1,0:T(8,128)(2,1)S(1)} %get-tuple-element.40), channel_id=1, source_target_pairs={{0,4},{1,5},{2,6},{3,7},{4,0},{5,1},{6,2},{7,3},{8,12},{9,13},{10,... | collective-permute-start | bytes 393224 | tf_op jit(solution)/shard_map/ppermute | solution.py:415
  76.9 3.8 %collective-permute-done.16 = bf16[8,8192]{1,0:T(8,128)(2,1)S(1)} collective-permute-done((bf16[8,8192]{1,0:T(8,128)(2,1)S(1)}, bf16[8,8192]{1,0:T(8,128)(2,1)S(1)}, u32[]{:S(2)}, u32[]{:S(2)}) %collective-permute-start.16) | collective-permute-done | bytes 131104 | tf_op jit(solution)/shard_map/ppermute | solution.py:415
  (26 shorter events, 10.7 us)
Async XLA Ops:
  0.9 8.9 %collective-permute-start.2 = (bf16[528,128]{1,0:T(8,128)(2,1)S(1)}, bf16[528,128]{1,0:T(8,128)(2,1)S(1)}, u32[]{:S(2)}, u32[]{:S(2)}) collective-permute-start(bf16[528,128]{1,0:T(8,128)(2,1)S(1)} %pack.1), channel_id=1, source_target_pairs={{0,24},{1,97},{2,26},{3,99},{4,28},{5,101},{6,30},{7,103},{8,0},{9... | collective-permute-start | bytes 405512 | tf_op jit(solution)/shard_map/ppermute | solution.py:372
  4.6 5.5 %collective-permute-start.1 = (bf16[528,128]{1,0:T(8,128)(2,1)S(1)}, bf16[528,128]{1,0:T(8,128)(2,1)S(1)}, u32[]{:S(2)}, u32[]{:S(2)}) collective-permute-start(bf16[528,128]{1,0:T(8,128)(2,1)S(1)} %pack.1), channel_id=1, source_target_pairs={{0,16},{1,65},{2,18},{3,67},{4,20},{5,69},{6,22},{7,71},{8,24},{9,... | collective-permute-start | bytes 405512 | tf_op jit(solution)/shard_map/ppermute | solution.py:372
  4.9 6.8 %collective-permute-start = (bf16[528,128]{1,0:T(8,128)(2,1)S(1)}, bf16[528,128]{1,0:T(8,128)(2,1)S(1)}, u32[]{:S(2)}, u32[]{:S(2)}) collective-permute-start(bf16[528,128]{1,0:T(8,128)(2,1)S(1)} %pack.1), channel_id=1, source_target_pairs={{0,8},{1,33},{2,10},{3,35},{4,12},{5,37},{6,14},{7,39},{8,16},{9,4... | collective-permute-start | bytes 405512 | tf_op jit(solution)/shard_map/ppermute | solution.py:372
  5.6 0.7 copy-start
  11.7 10.6 %collective-permute-start.3 = (bf16[4,528,128]{2,1,0:T(8,128)(2,1)S(1)}, bf16[4,528,128]{2,1,0:T(8,128)(2,1)S(1)}, u32[]{:S(2)}, u32[]{:S(2)}) collective-permute-start(bf16[4,528,128]{2,1,0:T(8,128)(2,1)S(1)} %pad_maximum_fusion.q_ref), channel_id=1, source_target_pairs={{0,32},{1,9},{2,34},{3,11},{4,36},{5,13},{6,38},{7,15},{8,40},{9,1... | collective-permute-start | bytes 1622024 | tf_op jit(solution)/shard_map/ppermute | solution.py:372
  13.2 16.1 %collective-permute-start.5 = (bf16[4,528,128]{2,1,0:T(8,128)(2,1)S(1)}, bf16[4,528,128]{2,1,0:T(8,128)(2,1)S(1)}, u32[]{:S(2)}, u32[]{:S(2)}) collective-permute-start(bf16[4,528,128]{2,1,0:T(8,128)(2,1)S(1)} %pad_maximum_fusion.q_ref), channel_id=1, source_target_pairs={{0,96},{1,25},{2,98},{3,27},{4,100},{5,29},{6,102},{7,31},{8,104},... | collective-permute-start | bytes 1622024 | tf_op jit(solution)/shard_map/ppermute | solution.py:372
  19.7 14.7 %collective-permute-start.7 = (bf16[4,528,128]{2,1,0:T(8,128)(2,1)S(1)}, bf16[4,528,128]{2,1,0:T(8,128)(2,1)S(1)}, u32[]{:S(2)}, u32[]{:S(2)}) collective-permute-start(bf16[4,528,128]{2,1,0:T(8,128)(2,1)S(1)} %pad_maximum_fusion.q_ref), channel_id=1, source_target_pairs={{0,64},{1,17},{2,66},{3,19},{4,68},{5,21},{6,70},{7,23},{8,72},{9,... | collective-permute-start | bytes 1622024 | tf_op jit(solution)/shard_map/ppermute | solution.py:372
  26.6 14.4 %collective-permute-start.4 = (bf16[4,528,128]{2,1,0:T(8,128)(2,1)S(1)}, bf16[4,528,128]{2,1,0:T(8,128)(2,1)S(1)}, u32[]{:S(2)}, u32[]{:S(2)}) collective-permute-start(bf16[4,528,128]{2,1,0:T(8,128)(2,1)S(1)} %attend.5), channel_id=1, source_target_pairs={{0,96},{1,25},{2,98},{3,27},{4,100},{5,29},{6,102},{7,31},{8,104},... | collective-permute-start | bytes 1622024 | tf_op jit(solution)/shard_map/ppermute | solution.py:372
  32.7 9.8 %collective-permute-start.6 = (bf16[4,528,128]{2,1,0:T(8,128)(2,1)S(1)}, bf16[4,528,128]{2,1,0:T(8,128)(2,1)S(1)}, u32[]{:S(2)}, u32[]{:S(2)}) collective-permute-start(bf16[4,528,128]{2,1,0:T(8,128)(2,1)S(1)} %attend.6), channel_id=1, source_target_pairs={{0,32},{1,9},{2,34},{3,11},{4,36},{5,13},{6,38},{7,15},{8,40},{9,1... | collective-permute-start | bytes 1622024 | tf_op jit(solution)/shard_map/ppermute | solution.py:372
  37.8 7.8 %collective-permute-start.9 = (bf16[2,528,128]{2,1,0:T(8,128)(2,1)S(1)}, bf16[2,528,128]{2,1,0:T(8,128)(2,1)S(1)}, u32[]{:S(2)}, u32[]{:S(2)}) collective-permute-start(bf16[2,528,128]{2,1,0:T(8,128)(2,1)S(1)} %get-tuple-element.32), channel_id=1, source_target_pairs={{0,64},{1,17},{2,66},{3,19},{4,68},{5,21},{6,70},{7,23},{8,72},{9,... | collective-permute-start | bytes 811016 | tf_op jit(solution)/shard_map/ppermute | solution.py:372
  41.0 12.0 %collective-permute-start.8 = (bf16[2,528,128]{2,1,0:T(8,128)(2,1)S(1)}, bf16[2,528,128]{2,1,0:T(8,128)(2,1)S(1)}, u32[]{:S(2)}, u32[]{:S(2)}) collective-permute-start(bf16[2,528,128]{2,1,0:T(8,128)(2,1)S(1)} %get-tuple-element.30), channel_id=1, source_target_pairs={{0,64},{1,17},{2,66},{3,19},{4,68},{5,21},{6,70},{7,23},{8,72},{9,... | collective-permute-start | bytes 811016 | tf_op jit(solution)/shard_map/ppermute | solution.py:372
  46.2 8.4 %collective-permute-start.10 = (bf16[528,128]{1,0:T(8,128)(2,1)S(1)}, bf16[528,128]{1,0:T(8,128)(2,1)S(1)}, u32[]{:S(2)}, u32[]{:S(2)}) collective-permute-start(bf16[528,128]{1,0:T(8,128)(2,1)S(1)} %get-tuple-element.33), channel_id=1, source_target_pairs={{0,24},{1,97},{2,26},{3,99},{4,28},{5,101},{6,30},{7,103},{8,0},{9... | collective-permute-start | bytes 405512 | tf_op jit(solution)/shard_map/ppermute | solution.py:372
  51.4 5.4 %collective-permute-start.11 = (bf16[528,128]{1,0:T(8,128)(2,1)S(1)}, bf16[528,128]{1,0:T(8,128)(2,1)S(1)}, u32[]{:S(2)}, u32[]{:S(2)}) collective-permute-start(bf16[528,128]{1,0:T(8,128)(2,1)S(1)} %get-tuple-element.34), channel_id=1, source_target_pairs={{0,16},{1,65},{2,18},{3,67},{4,20},{5,69},{6,22},{7,71},{8,24},{9,... | collective-permute-start | bytes 405512 | tf_op jit(solution)/shard_map/ppermute | solution.py:372
  53.6 5.7 %collective-permute-start.12 = (bf16[528,128]{1,0:T(8,128)(2,1)S(1)}, bf16[528,128]{1,0:T(8,128)(2,1)S(1)}, u32[]{:S(2)}, u32[]{:S(2)}) collective-permute-start(bf16[528,128]{1,0:T(8,128)(2,1)S(1)} %get-tuple-element.35), channel_id=1, source_target_pairs={{0,8},{1,33},{2,10},{3,35},{4,12},{5,37},{6,14},{7,39},{8,16},{9,4... | collective-permute-start | bytes 405512 | tf_op jit(solution)/shard_map/ppermute | solution.py:372
  66.3 4.5 %collective-permute-start.13 = (bf16[32,8192]{1,0:T(8,128)(2,1)S(1)}, bf16[32,8192]{1,0:T(8,128)(2,1)S(1)}, u32[]{:S(2)}, u32[]{:S(2)}) collective-permute-start(bf16[32,8192]{1,0:T(8,128)(2,1)S(1)} %get-tuple-element.38), channel_id=1, source_target_pairs={{0,1},{1,0},{2,3},{3,2},{4,5},{5,4},{6,7},{7,6},{8,9},{9,8},{10,11... | collective-permute-start | bytes 1572872 | tf_op jit(solution)/shard_map/ppermute | solution.py:407
  70.9 6.0 %collective-permute-start.14 = (bf16[8,8192]{1,0:T(8,128)(2,1)S(1)}, bf16[8,8192]{1,0:T(8,128)(2,1)S(1)}, u32[]{:S(2)}, u32[]{:S(2)}) collective-permute-start(bf16[8,8192]{1,0:T(8,128)(2,1)S(1)} %get-tuple-element.39), channel_id=1, source_target_pairs={{0,2},{1,3},{2,4},{3,5},{4,6},{5,7},{6,0},{7,1},{8,10},{9,11},{10,... | collective-permute-start | bytes 393224 | tf_op jit(solution)/shard_map/ppermute | solution.py:415
  72.2 8.5 %collective-permute-start.16 = (bf16[8,8192]{1,0:T(8,128)(2,1)S(1)}, bf16[8,8192]{1,0:T(8,128)(2,1)S(1)}, u32[]{:S(2)}, u32[]{:S(2)}) collective-permute-start(bf16[8,8192]{1,0:T(8,128)(2,1)S(1)} %get-tuple-element.40), channel_id=1, source_target_pairs={{0,4},{1,5},{2,6},{3,7},{4,0},{5,1},{6,2},{7,3},{8,12},{9,13},{10,... | collective-permute-start | bytes 393224 | tf_op jit(solution)/shard_map/ppermute | solution.py:415
  74.6 6.1 %collective-permute-start.15 = (bf16[8,8192]{1,0:T(8,128)(2,1)S(1)}, bf16[8,8192]{1,0:T(8,128)(2,1)S(1)}, u32[]{:S(2)}, u32[]{:S(2)}) collective-permute-start(bf16[8,8192]{1,0:T(8,128)(2,1)S(1)} %get-tuple-element.41), channel_id=1, source_target_pairs={{0,6},{1,7},{2,0},{3,1},{4,2},{5,3},{6,4},{7,5},{8,14},{9,15},{10,... | collective-permute-start | bytes 393224 | tf_op jit(solution)/shard_map/ppermute | solution.py:415
